TPU v7x, 256 devices: a whole 4x4x8 slice. The times are simulated.
256 devices in a mesh: seq: 64 (over z, y, core), head: 4 (over x).
Axes of the slice: x: 4, y: 4, z: 8, core: 2. Of those that a mesh axis runs over, the one named last changes fastest.
Arguments:
- latents: bfloat16 [128, 256, 64], P('seq'), may hold values from -6 to 6
- clip_ids: int32 [128], P('seq'), may hold values from 0 to 31, never falling along the last dimension, each value on 1 to 8 neighbouring positions
- owners: int32 [128], P('seq'), may hold values from 0 to 63, as said below
- slots: int32 [128], P('seq'), may hold values from 0 to 3, as said below
- extents: int32 [32, 2], replicated, may hold values from 8 to 48
- embed_weight: bfloat16 [64, 3072], replicated, may hold values from -0.75 to 0.75
- embed_bias: float32 [3072], replicated, may hold values from -3 to 3
- shift_table: bfloat16 [32, 3072], replicated, may hold values from -3 to 3
- scale_table: bfloat16 [32, 3072], replicated, may hold values from -1.796875 to 1.796875
- query_weight: bfloat16 [3072, 3072], P(None, 'head'), may hold values from -0.109375 to 0.109375
- key_weight: bfloat16 [3072, 3072], P(None, 'head'), may hold values from -0.109375 to 0.109375
- query_gain: float32 [128], replicated, may hold values from 0.1 to 1.9
- key_gain: float32 [128], replicated, may hold values from 0.1 to 1.9
Outputs:
- query_out: bfloat16 [65536, 3072], P('seq', 'head')
- key_out: bfloat16 [65536, 3072], P('seq', 'head')
Inputs may be any that keep to these rules, and one draw needn't show every extreme that they name: `clip_ids`: clip ids never fall along the blocks, and each clip has 1 to 8 blocks. The 2 blocks of one index of seq go to different owners; an owner receives at most 4 blocks, and some owner receives exactly 4. `slots`: no two blocks share both owner and slot.
All inputs are finite; a program needn't handle non-finite values.
Results may differ from a plain program's by a relative error of at most 0.0049.
Values may be sent and summed in bfloat16 or wider, within the bound.
A program may use at most 128 MiB of HBM per device.

v0:
```python
import jax
import jax.numpy as jnp
from jax import lax
from jax.sharding import PartitionSpec as P


def copy_for_each(x, axis):
    length = lax.axis_size(axis)
    return lax.all_to_all(jnp.broadcast_to(x[None], (length, *x.shape)), axis, 0, 0, tiled=True)


def collected_together(x, axis):
    leaves = jax.tree.leaves(x)
    sequence = sorted(range(len(leaves)), key=lambda k: -leaves[k].size)
    width = (1, *leaves[sequence[0]].shape)[-1]
    lines = [
        jnp.pad(leaves[k].reshape(-1), (0, -leaves[k].size % width)).reshape(-1, width)
        for k in sequence
    ]
    both, at, found = (copy_for_each(jnp.concatenate(lines), axis), 0, {})
    for k, line in zip(sequence, lines):
        share = both[:, at : at + len(line)].reshape(len(both), -1)
        found[k] = share[:, : leaves[k].size].reshape(-1, *leaves[k].shape)
        at += len(line)
    numbers = iter(range(len(leaves)))
    return jax.tree.map(lambda _: found[next(numbers)], x)


def combined_pairwise(pieces, combine):
    while len(jax.tree.leaves(pieces)[0]) > 1:
        pieces = jax.vmap(combine)(
            *(jax.tree.map(lambda part: part[side::2], pieces) for side in (0, 1))
        )
    return jax.tree.map(lambda part: part[0], pieces)


def entering(x, axis, combine, identity):
    length, mine = (lax.axis_size(axis), lax.axis_index(axis))
    passed = jnp.arange(length) < mine

    def kept(part, zero, own):
        part = jnp.where(
            passed.reshape(-1, *(1 for _ in own.shape)), part, jnp.asarray(zero, own.dtype)
        )
        return part

    pieces = collected_together(x, axis)
    return combined_pairwise(jax.tree.map(kept, pieces, identity, x), combine)


def shortened(x):
    return jax.tree.map(lambda a: a.astype(jnp.bfloat16) if a.dtype == jnp.float32 else a, x)


def token_angles(offsets, heights, widths, block_tokens):
    within = offsets[:, None] + jnp.arange(block_tokens, dtype=jnp.int32)[None, :]
    plane_size = heights * widths
    frames = within // plane_size[:, None]
    row_pos = within // widths[:, None] % heights[:, None]
    col_pos = within % widths[:, None]
    pieces = []
    for position, axis_width in ((frames, 16), (row_pos, 56), (col_pos, 56)):
        frequency = 1.0 / 10000.0 ** (jnp.arange(0, axis_width, 2, dtype=jnp.float32) / axis_width)
        pieces.append(position.reshape(-1).astype(jnp.float32)[:, None] * frequency[None, :])
    return jnp.concatenate(pieces, axis=1)


def finish(values, gains, angles):
    row_count, column_count = values.shape
    head_size = gains.shape[0]
    head_count = column_count // head_size
    grouped = values.reshape(row_count, head_count, head_size)
    inverse = lax.rsqrt(jnp.mean(grouped * grouped, axis=2, keepdims=True) + 1e-06)
    normed = grouped * inverse * gains
    paired = normed.reshape(row_count, head_count, head_size // 2, 2)
    even_part = paired[..., 0]
    odd_part = paired[..., 1]
    cosines = jnp.cos(angles)[:, None, :]
    sines = jnp.sin(angles)[:, None, :]
    turned = jnp.stack(
        [even_part * cosines - odd_part * sines, even_part * sines + odd_part * cosines], axis=-1
    )
    return turned.reshape(row_count, column_count).astype(jnp.bfloat16)


def project(
    latent,
    shift_rows,
    scale_rows,
    angles,
    embed_weight,
    embed_bias,
    query_weight,
    key_weight,
    query_gain,
    key_gain,
):
    block_count, token_count, channels = latent.shape
    hidden = (
        jnp.dot(
            latent.reshape(block_count * token_count, channels),
            embed_weight,
            preferred_element_type=jnp.float32,
        )
        + embed_bias
    )
    average = jnp.mean(hidden, axis=1, keepdims=True)
    centred = hidden - average
    variance = jnp.mean(centred * centred, axis=1, keepdims=True)
    normed = (centred * lax.rsqrt(variance + 1e-06)).reshape(block_count, token_count, -1)
    modulated = normed * (1.0 + scale_rows[:, None, :]) + shift_rows[:, None, :]
    modulated = modulated.astype(jnp.bfloat16).reshape(block_count * token_count, -1)
    queries = jnp.dot(modulated, query_weight, preferred_element_type=jnp.float32)
    key_rows = jnp.dot(modulated, key_weight, preferred_element_type=jnp.float32)
    return (finish(queries, query_gain, angles), finish(key_rows, key_gain, angles))


def join_runs(earlier, later):
    first_count, first_clip, first_trail = earlier
    next_count, next_clip, next_trail = later
    joined = (next_trail == next_count) & (first_clip == next_clip)
    trailing = next_trail + jnp.where(joined, first_trail, 0)
    present = next_count > 0
    return (
        first_count + next_count,
        jnp.where(present, next_clip, first_clip),
        jnp.where(present, trailing, first_trail),
    )


def per_device(
    latents,
    clip_ids,
    owners,
    slots,
    extents,
    embed_weight,
    embed_bias,
    shift_table,
    scale_table,
    query_weight,
    key_weight,
    query_gain,
    key_gain,
):
    local_blocks, block_tokens, channels = latents.shape
    ranks = lax.axis_size("seq")
    own_slots = 2 * local_blocks
    block_order = lax.iota(jnp.int32, local_blocks)
    same_before = jnp.sum(
        (
            (clip_ids[None, :] == clip_ids[:, None]) & (block_order[None, :] < block_order[:, None])
        ).astype(jnp.int32),
        axis=1,
    )
    final_clip = clip_ids[local_blocks - 1 :]
    trail_here = jnp.sum((clip_ids == final_clip[0]).astype(jnp.int32)).reshape(1)
    blocks_here = jnp.full((1,), local_blocks, jnp.int32)
    empty = (jnp.zeros((1,), jnp.int32), jnp.full((1,), -1, jnp.int32), jnp.zeros((1,), jnp.int32))
    prior_count, prior_clip, prior_trail = entering(
        (blocks_here, final_clip, trail_here), "seq", join_runs, empty
    )
    offsets = (same_before + jnp.where(clip_ids == prior_clip[0], prior_trail[0], 0)) * block_tokens
    quarter = block_tokens // lax.axis_size("head")
    portion = lax.dynamic_slice_in_dim(latents, lax.axis_index("head") * quarter, quarter, 1)
    tokens_here = portion.shape[1]
    flat_rows = portion.reshape(local_blocks, tokens_here * channels)
    block_info = jnp.stack([owners, slots, clip_ids, offsets, jnp.ones_like(owners)], axis=1)
    slot_order = lax.iota(jnp.int32, own_slots)
    target = owners[:, None] == lax.iota(jnp.int32, ranks)[None, :]
    send_rows = jnp.dot(
        target.T.astype(jnp.bfloat16), flat_rows, preferred_element_type=jnp.float32
    ).astype(jnp.bfloat16)
    send_info = jnp.sum(target.astype(jnp.int32)[:, :, None] * block_info[:, None, :], axis=0)
    got_rows, got_info = (
        lax.all_to_all(send_rows, "seq", split_axis=0, concat_axis=0, tiled=True),
        lax.all_to_all(shortened(send_info), "seq", split_axis=0, concat_axis=0, tiled=True).astype(
            send_info.dtype
        ),
    )
    chosen = (got_info[:, 4][None, :] == 1) & (got_info[:, 1][None, :] == slot_order[:, None])
    slot_rows = jnp.dot(chosen.astype(jnp.bfloat16), got_rows, preferred_element_type=jnp.float32)
    slot_info = jnp.sum(chosen.astype(jnp.int32)[:, :, None] * got_info[None, :, 2:], axis=1)
    slot_latent = slot_rows.astype(jnp.bfloat16).reshape(own_slots, tokens_here, channels)
    slot_latent = lax.all_gather(slot_latent, "head", axis=1, tiled=True)
    slot_clip = slot_info[:, 0]
    slot_offset = slot_info[:, 1]
    slot_used = slot_info[:, 2]
    clip_match = slot_clip[:, None] == lax.iota(jnp.int32, shift_table.shape[0])[None, :]
    heights = jnp.sum(jnp.where(clip_match, extents[:, 0][None, :], 0), axis=1)
    widths = jnp.sum(jnp.where(clip_match, extents[:, 1][None, :], 0), axis=1)
    selector = clip_match.astype(jnp.bfloat16)
    shift_rows = jnp.dot(selector, shift_table, preferred_element_type=jnp.float32)
    scale_rows = jnp.dot(selector, scale_table, preferred_element_type=jnp.float32)
    angles = token_angles(slot_offset, heights, widths, block_tokens)
    queries, key_rows = project(
        slot_latent,
        shift_rows,
        scale_rows,
        angles,
        embed_weight,
        embed_bias,
        query_weight,
        key_weight,
        query_gain,
        key_gain,
    )
    live_rows = jnp.repeat(slot_used, block_tokens)[:, None] > 0
    query_out = jnp.where(live_rows, queries, jnp.zeros_like(queries))
    key_out = jnp.where(live_rows, key_rows, jnp.zeros_like(key_rows))
    return (query_out, key_out)


def solution(mesh):
    placed = (
        P("seq", None, None),
        P("seq"),
        P("seq"),
        P("seq"),
        P(),
        P(),
        P(),
        P(),
        P(),
        P(None, "head"),
        P(None, "head"),
        P(),
        P(),
    )
    return jax.shard_map(
        per_device,
        mesh=mesh,
        in_specs=placed,
        out_specs=(P("seq", "head"), P("seq", "head")),
        check_vma=False,
    )
```

profile of v0, /device:TPU:1, one launch (start us, length us, event | category | flops | bytes accessed | tf_op | source)
XLA Modules:
  0.0 182.4 jit_solution(7519703270643433691)
XLA Ops:
  0.6 1.3 slice.158
  1.9 1.9 %fusion.41 = s32[]{:T(128)} fusion(s32[2]{0:T(128)} %param.18, s32[]{:T(128)} %bitcast.4), kind=kLoop, calls=%fused_computation.110 | loop fusion | flops 5 | bytes 16 | tf_op jit(solution)/shard_map/reduce_sum | solution.py:157
  3.9 1.4 add_bitcast_fusion
  5.9 13.1 %all-to-all-start = ((s32[64,3,1]{1,2,0:T(1,128)}), s32[64,3,1]{1,2,0:T(1,128)S(1)}, u32[]{:S(2)}, u32[]{:S(2)}) async-start(s32[64,3,1]{1,2,0:T(1,128)} %broadcast_in_dim.78), calls=%async_computation | async-start | bytes 65536 | tf_op jit(solution)/shard_map/all_to_all | solution.py:9
  21.7 1.1 fusion.5
  23.6 4.8 %all-to-all-done = s32[64,3,1]{1,2,0:T(1,128)S(1)} async-done(((s32[64,3,1]{1,2,0:T(1,128)}), s32[64,3,1]{1,2,0:T(1,128)S(1)}, u32[]{:S(2)}, u32[]{:S(2)}) %all-to-all-start) | async-done | bytes 800 | tf_op jit(solution)/shard_map/all_to_all | solution.py:9
  28.4 3.6 %slice_reduce_fusion.2 = (s32[64]{0:T(128)S(1)}, s32[64]{0:T(128)S(1)}, s32[64]{0:T(128)S(1)}) fusion(s32[64,3,1]{1,2,0:T(1,128)S(1)} %all-to-all-done), kind=kLoop, calls=%fused_computation.35 | loop fusion | bytes 1536 | tf_op jit(solution)/shard_map/slice | solution.py:22
  45.3 5.5 %all-to-all-start.1 = ((s32[64,1,5]{2,1,0:T(1,128)}), s32[64,1,5]{2,1,0:T(1,128)S(1)}, u32[]{:S(2)}, u32[]{:S(2)}) async-start(s32[64,1,5]{2,1,0:T(1,128)} %copy.71), calls=%async_computation.1 | async-start | bytes 65536 | tf_op jit(solution)/shard_map/all_to_all | solution.py:177
  51.3 1.0 reduce.10
  52.3 1.2 reshape.362
  53.5 6.7 %copy.75 = bf16[3072,768]{0,1:T(8,128)(2,1)} copy(bf16[3072,768]{1,0:T(8,128)(2,1)} %param.26) | data formatting | bytes 9437184 | tf_op args[9]
  60.2 6.7 %copy.76 = bf16[3072,768]{0,1:T(8,128)(2,1)} copy(bf16[3072,768]{1,0:T(8,128)(2,1)} %param.27) | data formatting | bytes 9437184 | tf_op args[10]
  66.9 10.4 %all-to-all-start.2 = ((bf16[64,2,2048]{2,1,0:T(2,128)(2,1)}), bf16[64,2,2048]{2,1,0:T(2,128)(2,1)S(1)}, u32[]{:S(2)}, u32[]{:S(2)}) async-start(bf16[64,2,2048]{2,1,0:T(2,128)(2,1)} %reshape.362), calls=%async_computation.2 | async-start | bytes 1048576 | tf_op jit(solution)/shard_map/all_to_all | solution.py:176
  79.0 1.7 fusion.9
  81.2 13.8 %all-to-all-done.2 = bf16[64,2,2048]{2,1,0:T(2,128)(2,1)S(1)} async-done(((bf16[64,2,2048]{2,1,0:T(2,128)(2,1)}), bf16[64,2,2048]{2,1,0:T(2,128)(2,1)S(1)}, u32[]{:S(2)}, u32[]{:S(2)}) %all-to-all-start.2) | async-done | bytes 524320 | tf_op jit(solution)/shard_map/all_to_all | solution.py:176
  96.3 10.4 %all_gather.3 = bf16[4,256,64]{2,1,0:T(8,128)(2,1)S(1)} all-gather(bf16[4,64,64]{2,1,0:T(8,128)(2,1)S(1)} %reshape.352), channel_id=1, replica_groups=mesh['seq'=64,'head'=4] {'head'}, dimensions={1}, use_global_device_ids=true | all-gather | bytes 163840 | tf_op jit(solution)/shard_map/all_gather | solution.py:185
  106.7 1.9 %add_reduce_fusion = (f32[1024]{0:T(1024)S(1)}, f32[1024,3072]{1,0:T(8,128)S(1)}) fusion(f32[3072]{0:T(1024)S(1)} %copy-done.5, bf16[1024,64]{1,0:T(8,128)(2,1)S(1)} %bitcast.124, bf16[64,3072]{1,0:T(8,128)(2,1)S(1)} %copy-done), kind=kOutput, calls=%fused_computation.4 | convolution fusion | flops 408943616 | bytes 13123584 | tf_op jit(solution)/shard_map/dot_general | solution.py:100
  108.6 1.8 multiply_reduce_fusion
  110.4 2.7 %copy-done.2 = f32[1024,3072]{1,0:T(8,128)} copy-done((f32[1024,3072]{1,0:T(8,128)}, f32[1024,3072]{1,0:T(8,128)S(1)}, u32[]{:S(2)}) %copy-start.2) | copy-done | bytes 12582936
  113.2 10.6 %fusion = bf16[1024,3072]{1,0:T(8,128)(2,1)} fusion(f32[1024,3072]{1,0:T(8,128)} %copy-done.2, f32[4,3072]{1,0:T(4,128)S(1)} %fusion.26, f32[4,3072]{1,0:T(4,128)S(1)} %convolution_add_fusion, f32[1024]{0:T(1024)S(1)} %add_rsqrt_fusion.2, f32[1024]{0:T(1024)S(1)} %broadcast_multiply_fusion.3, f32[3072]{0:T(1024)S(1)} %copy-done.5), kind=kLoop, calls=%fused_computation.1 | loop fusion | flops 18874368 | bytes 18993152 | tf_op jit(solution)/shard_map/convert_element_type | solution.py:112
  123.7 8.6 %multiply_reduce_fusion.2 = (f32[1024,6]{0,1:T(8,128)S(1)}, f32[1024,6,128]{0,2,1:T(8,128)S(1)}) fusion(bf16[6,128,3072]{2,1,0:T(8,128)(2,1)} %bitcast.123, bf16[1024,3072]{1,0:T(8,128)(2,1)} %fusion), kind=kOutput, calls=%fused_computation.16 | convolution fusion | flops 4833404928 | bytes 14180352 | tf_op jit(solution)/shard_map/dot_general | solution.py:113
  133.1 3.2 %reshape.354 = f32[1024,6,64,2]{0,3,2,1:T(2,128)} reshape(f32[1024,6,128]{0,2,1:T(8,128)S(1)} %multiply_multiply_fusion.1) | data formatting | bytes 6291456 | tf_op jit(solution)/shard_map/reshape | solution.py:75
  136.4 8.6 %multiply_reduce_fusion.1 = (f32[1024,6]{0,1:T(8,128)S(1)}, f32[1024,6,128]{0,2,1:T(8,128)S(1)}) fusion(bf16[6,128,3072]{2,1,0:T(8,128)(2,1)} %bitcast.122, bf16[1024,3072]{1,0:T(8,128)(2,1)} %fusion), kind=kOutput, calls=%fused_computation.14 | convolution fusion | flops 4833404928 | bytes 14180352 | tf_op jit(solution)/shard_map/dot_general | solution.py:114
  145.8 3.3 %reshape.355 = f32[1024,6,64,2]{0,3,2,1:T(2,128)} reshape(f32[1024,6,128]{0,2,1:T(8,128)S(1)} %multiply_multiply_fusion) | data formatting | bytes 6291456 | tf_op jit(solution)/shard_map/reshape | solution.py:75
  149.1 10.2 %subtract_convert_fusion = (bf16[1024,6,64,1]{0,3,2,1:T(2,128)(2,1)S(1)}, bf16[1024,6,64,1]{0,3,2,1:T(2,128)(2,1)S(1)}, bf16[1024,6,64,1]{0,3,2,1:T(2,128)(2,1)S(1)}, bf16[1024,6,64,1]{0,3,2,1:T(2,128)(2,1)S(1)}) fusion(f32[1024,6,64,2]{0,3,2,1:T(2,128)} %reshape.355, f32[1024,64]{0,1:T(8,128)} %get-tuple-element.28, f32[1024,64]{0,1:T(8,128)S(1)} %copy-done.4, ...), kind=kLoop, calls=%fused_computation.20 | loop fusion | flops 6291456 | bytes 9961472 | tf_op jit(solution)/shard_map/convert
  159.2 4.4 %pad_maximum_fusion = bf16[1024,6,64,2]{0,3,2,1:T(2,128)(2,1)} fusion(bf16[1024,6,64,1]{0,3,2,1:T(2,128)(2,1)S(1)} %get-tuple-element.25, bf16[1024,6,64,1]{0,3,2,1:T(2,128)(2,1)S(1)} %get-tuple-element.26), kind=kLoop, calls=%fused_computation.17 | loop fusion | flops 3145728 | bytes 3145728 | tf_op jit(solution)/shard_map/stack | solution.py:80
  163.7 3.7 %convert_element_type.84 = bf16[1024,768]{0,1:T(8,128)(2,1)} reshape(bf16[1024,6,64,2]{0,3,2,1:T(2,128)(2,1)} %pad_maximum_fusion) | data formatting | bytes 3145728 | tf_op jit(solution)/shard_map/convert_element_type | solution.py:83
  167.3 4.4 %pad_maximum_fusion.1 = bf16[1024,6,64,2]{0,3,2,1:T(2,128)(2,1)} fusion(bf16[1024,6,64,1]{0,3,2,1:T(2,128)(2,1)S(1)} %get-tuple-element.22, bf16[1024,6,64,1]{0,3,2,1:T(2,128)(2,1)S(1)} %get-tuple-element.21), kind=kLoop, calls=%fused_computation.18 | loop fusion | flops 3145728 | bytes 3145728 | tf_op jit(solution)/shard_map/stack | solution.py:80
  171.7 3.8 %convert_element_type.85 = bf16[1024,768]{0,1:T(8,128)(2,1)} reshape(bf16[1024,6,64,2]{0,3,2,1:T(2,128)(2,1)} %pad_maximum_fusion.1) | data formatting | bytes 3145728 | tf_op jit(solution)/shard_map/convert_element_type | solution.py:83
  175.5 2.8 %broadcast_select_fusion = (bf16[1024,768]{0,1:T(8,128)(2,1)S(1)}, bf16[1024,768]{0,1:T(8,128)(2,1)}) fusion(bf16[1024,768]{0,1:T(8,128)(2,1)} %convert_element_type.85, pred[1024]{0:T(1024)(128)(4,1)S(1)} %gt.46, bf16[1024,768]{0,1:T(8,128)(2,1)S(1)} %copy-done.3), kind=kLoop, calls=%fused_computation.23 | loop fusion | flops 1572864 | bytes 6292480 | tf_op jit(solution)/shard_map/jit(_where)/select_n | solution.py:210
  178.2 2.6 %copy.77 = bf16[1024,768]{1,0:T(8,128)(2,1)} copy(bf16[1024,768]{0,1:T(8,128)(2,1)} %get-tuple-element.42) | data formatting | bytes 3145728
  180.9 1.6 copy.78
  (106 shorter events, 16.6 us)
Async XLA Ops:
  0.6 106.1 %copy-start = (bf16[64,3072]{1,0:T(8,128)(2,1)S(1)}, bf16[64,3072]{1,0:T(8,128)(2,1)}, u32[]{:S(2)}) copy-start(bf16[64,3072]{1,0:T(8,128)(2,1)} %param.22) | copy-start | bytes 1179652
  5.9 22.5 %all-to-all-start = ((s32[64,3,1]{1,2,0:T(1,128)}), s32[64,3,1]{1,2,0:T(1,128)S(1)}, u32[]{:S(2)}, u32[]{:S(2)}) async-start(s32[64,3,1]{1,2,0:T(1,128)} %broadcast_in_dim.78), calls=%async_computation | async-start | bytes 65536 | tf_op jit(solution)/shard_map/all_to_all | solution.py:9
  45.3 21.6 %all-to-all-start.1 = ((s32[64,1,5]{2,1,0:T(1,128)}), s32[64,1,5]{2,1,0:T(1,128)S(1)}, u32[]{:S(2)}, u32[]{:S(2)}) async-start(s32[64,1,5]{2,1,0:T(1,128)} %copy.71), calls=%async_computation.1 | async-start | bytes 65536 | tf_op jit(solution)/shard_map/all_to_all | solution.py:177
  60.2 20.6 %copy-start.6 = (bf16[32,3072]{1,0:T(8,128)(2,1)S(1)}, bf16[32,3072]{1,0:T(8,128)(2,1)}, u32[]{:S(2)}) copy-start(bf16[32,3072]{1,0:T(8,128)(2,1)} %param.25) | copy-start | bytes 589828
  60.2 20.8 %copy-start.7 = (bf16[32,3072]{1,0:T(8,128)(2,1)S(1)}, bf16[32,3072]{1,0:T(8,128)(2,1)}, u32[]{:S(2)}) copy-start(bf16[32,3072]{1,0:T(8,128)(2,1)} %param.24) | copy-start | bytes 589828
  66.9 39.9 %copy-start.5 = (f32[3072]{0:T(1024)S(1)}, f32[3072]{0:T(1024)}, u32[]{:S(2)}) copy-start(f32[3072]{0:T(1024)} %param.23) | copy-start | bytes 36868
  66.9 28.1 %all-to-all-start.2 = ((bf16[64,2,2048]{2,1,0:T(2,128)(2,1)}), bf16[64,2,2048]{2,1,0:T(2,128)(2,1)S(1)}, u32[]{:S(2)}, u32[]{:S(2)}) async-start(bf16[64,2,2048]{2,1,0:T(2,128)(2,1)} %reshape.362), calls=%async_computation.2 | async-start | bytes 1048576 | tf_op jit(solution)/shard_map/all_to_all | solution.py:176
  108.6 4.6 %copy-start.2 = (f32[1024,3072]{1,0:T(8,128)}, f32[1024,3072]{1,0:T(8,128)S(1)}, u32[]{:S(2)}) copy-start(f32[1024,3072]{1,0:T(8,128)S(1)} %get-tuple-element.65) | copy-start | bytes 37748740
  123.7 8.6 %copy-start.8 = (f32[128]{0:T(128)S(1)}, f32[128]{0:T(128)}, u32[]{:S(2)}) copy-start(f32[128]{0:T(128)} %param.28) | copy-start | bytes 1540
  136.4 8.6 %copy-start.9 = (f32[128]{0:T(128)S(1)}, f32[128]{0:T(128)}, u32[]{:S(2)}) copy-start(f32[128]{0:T(128)} %param.29) | copy-start | bytes 1540
  145.8 3.3 %copy-start.4 = (f32[1024,64]{0,1:T(8,128)S(1)}, f32[1024,64]{0,1:T(8,128)}, u32[]{:S(2)}) copy-start(f32[1024,64]{0,1:T(8,128)} %get-tuple-element.27) | copy-start | bytes 786436
  171.7 3.8 %copy-start.3 = (bf16[1024,768]{0,1:T(8,128)(2,1)S(1)}, bf16[1024,768]{0,1:T(8,128)(2,1)}, u32[]{:S(2)}) copy-start(bf16[1024,768]{0,1:T(8,128)(2,1)} %convert_element_type.84) | copy-start | bytes 4718596
  178.2 4.2 %copy-start.1 = (bf16[64,3072]{1,0:T(8,128)(2,1)S(1)}, bf16[64,3072]{1,0:T(8,128)(2,1)}, u32[]{:S(2)}) copy-start(bf16[64,3072]{1,0:T(8,128)(2,1)} %param.22) | copy-start | bytes 1179652
where the time goes:
time: 185 us; the launch traced here: 182 us
  local copies, waits for them, and re-layouts  50.6 us (27%)
  other arithmetic  45.4 us (25%)
  starting transfers between devices  29.1 us (16%)
  matrix products  21.2 us (11%)
  waiting for transfers between devices  18.6 us (10%)
  blocking collectives  10.4 us (6%)
  between operations  7.1 us (4%)
    unnamed x29, local copies, waits for them, and re-layouts  22 us
    all_to_all x1, waiting for transfers between devices, per_device(): lax.all_to_all(send_rows, 'seq', split_axis=0, concat_axis=0, tiled=True)  13.8 us
    all_to_all x1, starting transfers between devices, copy_for_each(): lax.all_to_all(jnp.broadcast_to(x[None], (length, *x.shape)), axis, 0, 0,...  13.1 us
    convert_element_type x1, other arithmetic, project(): modulated.astype(jnp.bfloat16).reshape(block_count * token_count, -1)  10.6 us
    all_to_all x1, starting transfers between devices, per_device(): lax.all_to_all(send_rows, 'seq', split_axis=0, concat_axis=0, tiled=True)  10.4 us
    all_gather x1, blocking collectives, per_device(): slot_latent = lax.all_gather(slot_latent, 'head', axis=1, tiled=True)  10.4 us
    another operation x1, other arithmetic  10.2 us
    another operation x2, other arithmetic, finish(): jnp.stack([even_part * cosines - odd_part * sines, even_part * sines + od...  8.81 us
  transfers between devices with their start and end apart: 3, of which 2 were waited for; matrix products, arithmetic and copies ran while one was open for 13% of the time, Pallas kernels for 0%

commit v1 on v0

v1 whole, which is shorter than its diff:
```python
import functools
import jax
import jax.numpy as jnp
import numpy as np
from jax import lax
from jax.experimental import pallas as pl
from jax.experimental.pallas import tpu as pltpu
from jax.sharding import PartitionSpec as P

F32, BF16, I32 = jnp.float32, jnp.bfloat16, jnp.int32
HIGH = lax.Precision.HIGHEST


def rope_table():
    table = np.zeros((128, 256), np.float32)
    row = lane = 0
    for places, width in ((32, 16), (48, 56), (48, 56)):
        rate = 1.0 / 10000.0 ** (np.arange(0, width, 2, dtype=np.float32) / np.float32(width))
        angle = np.arange(places, dtype=np.float32)[:, None] * rate[None, :].astype(np.float32)
        span = slice(lane, lane + width)
        table[row : row + places, span] = np.repeat(np.cos(angle), 2, axis=1)
        sines = np.repeat(np.sin(angle), 2, axis=1)
        sines[:, 0::2] *= -1.0
        table[row : row + places, 128 + lane : 128 + lane + width] = sines
        row, lane = row + places, lane + width
    return table


def lane_swapped(x):
    width = x.shape[-1]
    even = lax.broadcasted_iota(I32, x.shape, 1) % 2 == 0
    return jnp.where(even, pltpu.roll(x, width - 1, 1), pltpu.roll(x, 1, 1))


def halves(x):
    top = x.astype(BF16)
    return top, (x - top.astype(F32)).astype(BF16)


def finish_kernel(
    info, extents, xt, we, be, shift, scale, gq, gk, table, wq, wk,
    oq, ok,
    w, left, shift_f, scale_f, zz, cs, eps, out, w_sem, o_sem,
):
    slots, channels, tokens = xt.shape
    depth = we.shape[1]
    chunks, _, wide = w.shape
    per = chunks // 2

    def weight_copy(n):
        source = (wq if n < per else wk).at[:, pl.ds((n % per) * wide, wide)]
        return pltpu.make_async_copy(source, w.at[n], w_sem.at[n])

    for n in range(chunks):
        weight_copy(n).start()

    shift_f[...] = shift[...].astype(F32)
    scale_f[...] = scale[...].astype(F32)
    a = we[...].astype(F32)
    a = a - jnp.mean(a, axis=1, keepdims=True)
    b = be[...]
    b = b - jnp.mean(b, axis=1, keepdims=True)
    sub8 = lax.broadcasted_iota(I32, (8, depth), 0)
    b8 = jnp.where(sub8 == 0, b, 0.0)
    whole = jnp.concatenate([a, b8], axis=0)
    gram = lax.dot_general(
        whole, whole, (((1,), (1,)), ((), ())), precision=HIGH, preferred_element_type=F32
    ) * (1.0 / depth)

    extra = []
    for s in range(slots):
        clip = info[s, 0]
        gain = 1.0 + scale_f[pl.ds(clip, 1), :]
        left[pl.ds(s * channels, channels), :] = (a * gain).astype(BF16)
        move = shift_f[pl.ds(clip, 1), :]
        extra.append(jnp.where(sub8 == 0, b * gain, jnp.where(sub8 <= 2, move, 0.0)))
    left[pl.ds(slots * channels, 8 * slots), :] = jnp.concatenate(extra, axis=0).astype(BF16)

    lane = lax.broadcasted_iota(I32, (1, 128), 1)
    sub = lax.broadcasted_iota(I32, (8, tokens), 0)
    both = []
    for g in (gq, gk):
        gain = jnp.concatenate([g[...], lane_swapped(g[...])], axis=1)
        both.extend(halves(table[...] * gain))
    q_table = jnp.concatenate([both[0], both[1]], axis=0)
    k_table = jnp.concatenate([both[2], both[3]], axis=0)
    for s in range(slots):
        x = xt[s].astype(F32)
        x1 = jnp.concatenate([x, jnp.where(sub == 0, 1.0, 0.0)], axis=0)
        y = jnp.dot(gram, x1, precision=HIGH, preferred_element_type=F32)
        var = jnp.maximum(jnp.sum(y * x1, axis=0, keepdims=True), 0.0) + 1e-06
        dev = jnp.sqrt(var)
        dev_hi = dev.astype(BF16).astype(F32)
        more = jnp.where(
            sub == 0, 1.0,
            jnp.where(sub == 1, dev_hi,
                      jnp.where(sub == 2, dev - dev_hi, jnp.where(sub == 3, var * 1e-06, 0.0))),
        )
        zt = jnp.concatenate([x, more, jnp.zeros((128 - channels - 8, tokens), F32)], axis=0)
        z = zt.T
        zb = z.astype(BF16)
        zz[pl.ds(s * tokens, tokens), :] = jnp.concatenate([zb, zb], axis=1)
        eps[s] = jnp.broadcast_to(z[:, channels + 3 : channels + 4], (tokens, 128))
        clip = info[s, 0]
        high = jnp.full((1, 128), extents[clip, 0], I32).astype(F32)
        width = jnp.full((1, 128), extents[clip, 1], I32).astype(F32)
        index = (info[s, 1] + lax.broadcasted_iota(I32, (tokens, 128), 0)).astype(F32)
        frame = jnp.floor((index + 0.5) * (1.0 / (high * width)))
        line = jnp.floor((index + 0.5) * (1.0 / width))
        place = jnp.where(
            lane < 32, frame, jnp.where(lane < 80, line - high * frame + 32.0, index - width * line + 80.0)
        )
        hot = jnp.where(place == lane.astype(F32), 1.0, 0.0).astype(BF16)
        hot = jnp.concatenate([hot, hot], axis=1)
        cs[0, s] = jnp.dot(hot, q_table, preferred_element_type=F32)
        cs[1, s] = jnp.dot(hot, k_table, preferred_element_type=F32)

    r_i = lax.broadcasted_iota(I32, (wide, wide), 0) // 128
    c_i = lax.broadcasted_iota(I32, (wide, wide), 1) // 128
    ones = jnp.where(r_i == c_i, 1.0, 0.0).astype(BF16)
    empty = jnp.zeros((128 - channels - 8, wide), F32)

    def out_copies(n):
        return (
            pltpu.make_async_copy(out.at[n], oq.at[:, pl.ds((n % per) * wide, wide)], o_sem.at[n]),
            pltpu.make_async_copy(out.at[n], ok.at[:, pl.ds((n % per) * wide, wide)], o_sem.at[n]),
        )

    def stack(m, s):
        own = jnp.concatenate(
            [m[s * channels : (s + 1) * channels],
             m[slots * channels + 8 * s : slots * channels + 8 * s + 8], empty], axis=0)
        hi, lo = halves(own)
        return jnp.concatenate([hi, lo], axis=0)

    def chunk(n, carry):
        which = n // per
        pltpu.make_async_copy(wq.at[:, pl.ds(0, wide)], w.at[n], w_sem.at[n]).wait()
        m = jnp.dot(left[...], w[n], preferred_element_type=F32)
        turned = lane_swapped(m)
        for s in range(slots):
            z = zz[pl.ds(s * tokens, tokens), :]
            v = jnp.dot(z, stack(m, s), preferred_element_type=F32)
            vs = jnp.dot(z, stack(turned, s), preferred_element_type=F32)
            power = jnp.dot((v * v).astype(BF16), ones, preferred_element_type=F32)
            c = cs[which, s, :, 0:128]
            sn = cs[which, s, :, 128:256]
            e = eps[s]
            for h in range(wide // 128):
                at = slice(h * 128, (h + 1) * 128)
                inverse = lax.rsqrt(power[:, at] * (1.0 / 128.0) + e)
                o = (v[:, at] * c + vs[:, at] * sn) * inverse
                o = jnp.where(info[s, 2] > 0, o, 0.0)
                out[n, pl.ds(s * tokens, tokens), at] = o.astype(BF16)
        to_q, to_k = out_copies(n)

        @pl.when(n < per)
        def _():
            to_q.start()

        @pl.when(n >= per)
        def _():
            to_k.start()

        return carry

    lax.fori_loop(0, chunks, chunk, 0)
    for n in range(chunks):
        out_copies(n)[n // per].wait()


def finished(info, extents, xt, we, be, shift, scale, gq, gk, wq, wk):
    slots, channels, tokens = xt.shape
    clips, depth = shift.shape
    columns = wq.shape[1]
    wide = 256
    chunks = 2 * columns // wide
    rows = slots * tokens
    vmem = pl.BlockSpec(memory_space=pltpu.VMEM)
    smem = pl.BlockSpec(memory_space=pltpu.SMEM)
    hbm = pl.BlockSpec(memory_space=pl.ANY)
    return pl.pallas_call(
        finish_kernel,
        out_shape=[jax.ShapeDtypeStruct((rows, columns), BF16)] * 2,
        in_specs=[smem, smem] + [vmem] * 8 + [hbm, hbm],
        out_specs=[hbm, hbm],
        scratch_shapes=[
            pltpu.VMEM((chunks, depth, wide), BF16),
            pltpu.VMEM((slots * (channels + 8), depth), BF16),
            pltpu.VMEM((clips, depth), F32),
            pltpu.VMEM((clips, depth), F32),
            pltpu.VMEM((rows, 256), BF16),
            pltpu.VMEM((2, slots, tokens, 256), F32),
            pltpu.VMEM((slots, tokens, 128), F32),
            pltpu.VMEM((chunks, rows, wide), BF16),
            pltpu.SemaphoreType.DMA((chunks,)),
            pltpu.SemaphoreType.DMA((chunks,)),
        ],
        compiler_params=pltpu.CompilerParams(vmem_limit_bytes=60 << 20),
        name="finish",
    )(info, extents, xt, we, be.reshape(1, -1), shift, scale, gq.reshape(1, -1), gk.reshape(1, -1),
      jnp.asarray(rope_table()), wq, wk)


def copy_for_each(x, axis):
    length = lax.axis_size(axis)
    return lax.all_to_all(jnp.broadcast_to(x[None], (length, *x.shape)), axis, 0, 0, tiled=True)


def collected_together(x, axis):
    leaves = jax.tree.leaves(x)
    sequence = sorted(range(len(leaves)), key=lambda k: -leaves[k].size)
    width = (1, *leaves[sequence[0]].shape)[-1]
    lines = [
        jnp.pad(leaves[k].reshape(-1), (0, -leaves[k].size % width)).reshape(-1, width)
        for k in sequence
    ]
    both, at, found = (copy_for_each(jnp.concatenate(lines), axis), 0, {})
    for k, line in zip(sequence, lines):
        share = both[:, at : at + len(line)].reshape(len(both), -1)
        found[k] = share[:, : leaves[k].size].reshape(-1, *leaves[k].shape)
        at += len(line)
    numbers = iter(range(len(leaves)))
    return jax.tree.map(lambda _: found[next(numbers)], x)


def combined_pairwise(pieces, combine):
    while len(jax.tree.leaves(pieces)[0]) > 1:
        pieces = jax.vmap(combine)(
            *(jax.tree.map(lambda part: part[side::2], pieces) for side in (0, 1))
        )
    return jax.tree.map(lambda part: part[0], pieces)


def entering(x, axis, combine, identity):
    length, mine = (lax.axis_size(axis), lax.axis_index(axis))
    passed = jnp.arange(length) < mine

    def kept(part, zero, own):
        part = jnp.where(
            passed.reshape(-1, *(1 for _ in own.shape)), part, jnp.asarray(zero, own.dtype)
        )
        return part

    pieces = collected_together(x, axis)
    return combined_pairwise(jax.tree.map(kept, pieces, identity, x), combine)


def shortened(x):
    return jax.tree.map(lambda a: a.astype(jnp.bfloat16) if a.dtype == jnp.float32 else a, x)


def join_runs(earlier, later):
    first_count, first_clip, first_trail = earlier
    next_count, next_clip, next_trail = later
    joined = (next_trail == next_count) & (first_clip == next_clip)
    trailing = next_trail + jnp.where(joined, first_trail, 0)
    present = next_count > 0
    return (
        first_count + next_count,
        jnp.where(present, next_clip, first_clip),
        jnp.where(present, trailing, first_trail),
    )


def per_device(
    latents,
    clip_ids,
    owners,
    slots,
    extents,
    embed_weight,
    embed_bias,
    shift_table,
    scale_table,
    query_weight,
    key_weight,
    query_gain,
    key_gain,
):
    local_blocks, block_tokens, channels = latents.shape
    ranks = lax.axis_size("seq")
    own_slots = 2 * local_blocks
    block_order = lax.iota(jnp.int32, local_blocks)
    same_before = jnp.sum(
        (
            (clip_ids[None, :] == clip_ids[:, None]) & (block_order[None, :] < block_order[:, None])
        ).astype(jnp.int32),
        axis=1,
    )
    final_clip = clip_ids[local_blocks - 1 :]
    trail_here = jnp.sum((clip_ids == final_clip[0]).astype(jnp.int32)).reshape(1)
    blocks_here = jnp.full((1,), local_blocks, jnp.int32)
    empty = (jnp.zeros((1,), jnp.int32), jnp.full((1,), -1, jnp.int32), jnp.zeros((1,), jnp.int32))
    prior_count, prior_clip, prior_trail = entering(
        (blocks_here, final_clip, trail_here), "seq", join_runs, empty
    )
    offsets = (same_before + jnp.where(clip_ids == prior_clip[0], prior_trail[0], 0)) * block_tokens
    quarter = channels // lax.axis_size("head")
    portion = lax.dynamic_slice_in_dim(
        jnp.transpose(latents, (0, 2, 1)), lax.axis_index("head") * quarter, quarter, 1
    )
    flat_rows = portion.reshape(local_blocks, -1)
    block_info = jnp.stack([owners, slots, clip_ids, offsets, jnp.ones_like(owners)], axis=1)
    slot_order = lax.iota(jnp.int32, own_slots)
    target = owners[:, None] == lax.iota(jnp.int32, ranks)[None, :]
    send_rows = jnp.dot(
        target.T.astype(jnp.bfloat16), flat_rows, preferred_element_type=jnp.float32
    ).astype(jnp.bfloat16)
    send_info = jnp.sum(target.astype(jnp.int32)[:, :, None] * block_info[:, None, :], axis=0)
    got_rows, got_info = (
        lax.all_to_all(send_rows, "seq", split_axis=0, concat_axis=0, tiled=True),
        lax.all_to_all(shortened(send_info), "seq", split_axis=0, concat_axis=0, tiled=True).astype(
            send_info.dtype
        ),
    )
    chosen = (got_info[:, 4][None, :] == 1) & (got_info[:, 1][None, :] == slot_order[:, None])
    slot_rows = jnp.dot(chosen.astype(jnp.bfloat16), got_rows, preferred_element_type=jnp.float32)
    slot_info = jnp.sum(chosen.astype(jnp.int32)[:, :, None] * got_info[None, :, 2:], axis=1)
    slot_latent = slot_rows.astype(jnp.bfloat16).reshape(own_slots, quarter, block_tokens)
    slot_latent = lax.all_gather(slot_latent, "head", axis=1, tiled=True)
    slot_clip = slot_info[:, 0]
    slot_offset = slot_info[:, 1]
    slot_used = slot_info[:, 2]
    info = jnp.stack([slot_clip, slot_offset, slot_used], axis=1)
    return tuple(
        finished(
            info, extents, slot_latent, embed_weight, embed_bias, shift_table, scale_table,
            query_gain, key_gain, query_weight, key_weight,
        )
    )


def solution(mesh):
    placed = (
        P("seq", None, None),
        P("seq"),
        P("seq"),
        P("seq"),
        P(),
        P(),
        P(),
        P(),
        P(),
        P(None, "head"),
        P(None, "head"),
        P(),
        P(),
    )
    return jax.shard_map(
        per_device,
        mesh=mesh,
        in_specs=placed,
        out_specs=(P("seq", "head"), P("seq", "head")),
        check_vma=False,
    )
```

time: 185 us -> 113 us (0.61)
  other arithmetic: 45.4 us -> 7.09 us
  local copies, waits for them, and re-layouts: 50.6 us -> 16.4 us
  matrix products: 21.2 us -> 1.74 us
  Pallas kernels: 0 us -> 17.3 us
  waiting for transfers between devices: 18.6 us -> 28.4 us
  starting transfers between devices: 29.1 us -> 22.6 us
    dot_general x5 -> x0, matrix products: 19.5 us -> none  [the longest x1 8.62 us: project(): jnp.dot(modulated, key_weight, preferred_element_type=jnp.float32)]
    another operation x3 -> x0, other arithmetic: 19 us -> none
    unnamed x29 -> x8, local copies, waits for them, and re-layouts: 22 us -> 3.09 us
    pallas_call x0 -> x1, Pallas kernels: none -> 17.3 us  [finished(): pl.pallas_call(finish_kernel, out_shape=[jax.ShapeDtypeStruct((rows, colu...]
    convert_element_type x1 -> x0, other arithmetic: 10.6 us -> none  [project(): modulated.astype(jnp.bfloat16).reshape(block_count * token_count, -1)]
    convert_element_type x2 -> x0, local copies, waits for them, and re-layouts: 7.42 us -> none  [finish(): return turned.reshape(row_count, column_count).astype(jnp.bfloat16)]
    reshape x4 -> x0, local copies, waits for them, and re-layouts: 6.71 us -> none  [the longest x2 6.48 us: finish(): paired = normed.reshape(row_count, head_count, head_size // 2, 2)]
    all_to_all x1, starting transfers between devices: 10.4 us -> 4.74 us  [per_device(): lax.all_to_all(send_rows, 'seq', split_axis=0, concat_axis=0, tiled=True)]
  transfers between devices with their start and end apart: 3 -> 3, of which waited for: 2 -> 3; matrix products, arithmetic and copies ran while one was open for 13% -> 7% of each run, Pallas kernels for 0% -> 0%
where the time goes in v1:
time: 113 us; the launch traced here: 111 us
  waiting for transfers between devices  28.4 us (25%)
  starting transfers between devices  22.6 us (20%)
  Pallas kernels  17.3 us (15%)
  local copies, waits for them, and re-layouts  16.4 us (15%)
  blocking collectives  10.6 us (9%)
  other arithmetic  7.09 us (6%)
  between operations  7.08 us (6%)
  matrix products  1.74 us (2%)
    pallas_call x1, Pallas kernels, finished(): pl.pallas_call(finish_kernel, out_shape=[jax.ShapeDtypeStruct((rows, colu...  17.3 us
    all_to_all x1, waiting for transfers between devices, per_device(): lax.all_to_all(send_rows, 'seq', split_axis=0, concat_axis=0, tiled=True)  15.1 us
    all_to_all x1, starting transfers between devices, copy_for_each(): lax.all_to_all(jnp.broadcast_to(x[None], (length, *x.shape)), axis, 0, 0,...  13.1 us
    all_gather x1, blocking collectives, per_device(): slot_latent = lax.all_gather(slot_latent, 'head', axis=1, tiled=True)  10.6 us
    all_to_all x1, waiting for transfers between devices, copy_for_each(): lax.all_to_all(jnp.broadcast_to(x[None], (length, *x.shape)), axis, 0, 0,...  7.66 us
    all_to_all x1, waiting for transfers between devices, per_device(): lax.all_to_all(shortened(send_info), 'seq', split_axis=0, concat_axis=0,...  5.67 us
    slice x33, local copies, waits for them, and re-layouts, combined_pairwise(): part[side::2]  4.83 us
    all_to_all x1, starting transfers between devices, per_device(): lax.all_to_all(send_rows, 'seq', split_axis=0, concat_axis=0, tiled=True)  4.74 us
  transfers between devices with their start and end apart: 3, of which 3 were waited for; matrix products, arithmetic and copies ran while one was open for 7% of the time, Pallas kernels for 0%

profile of v1, /device:TPU:1, one launch (start us, length us, event | category | flops | bytes accessed | tf_op | source)
XLA Modules:
  0.0 111.2 jit_solution(1431971918822713647)
XLA Ops:
  0.6 1.3 %slice.135 = s32[1]{0:T(128)} slice(s32[2]{0:T(128)} %param.15), slice={[1:2]} | slice | bytes 8 | tf_op jit(solution)/shard_map/slice | solution.py:291
  1.9 1.9 %fusion.16 = s32[]{:T(128)} fusion(s32[2]{0:T(128)} %param.15, s32[]{:T(128)} %bitcast.4), kind=kLoop, calls=%fused_computation.46 | loop fusion | flops 5 | bytes 16 | tf_op jit(solution)/shard_map/reduce_sum | solution.py:292
  3.9 1.4 %add_bitcast_fusion = s32[3]{0:T(128)S(1)} fusion(s32[1,1]{0,1:T(1,128)} %bitcast.5, s32[1,1]{0,1:T(1,128)} %bitcast.3, s32[1,1]{0,1:T(1,128)} %constant.15.clone.1), kind=kLoop, calls=%fused_computation.48 | loop fusion | flops 6 | bytes 24 | tf_op jit(solution)/shard_map/broadcast_in_dim | solution.py:207
  5.2 0.6 broadcast_in_dim.61
  5.9 13.1 %all-to-all-start = ((s32[64,3,1]{1,2,0:T(1,128)}), s32[64,3,1]{1,2,0:T(1,128)S(1)}, u32[]{:S(2)}, u32[]{:S(2)}) async-start(s32[64,3,1]{1,2,0:T(1,128)} %broadcast_in_dim.61), calls=%async_computation | async-start | bytes 65536 | tf_op jit(solution)/shard_map/all_to_all | solution.py:207
  19.0 0.9 fusion.7
  19.9 0.7 fusion.9
  20.7 7.7 %all-to-all-done = s32[64,3,1]{1,2,0:T(1,128)S(1)} async-done(((s32[64,3,1]{1,2,0:T(1,128)}), s32[64,3,1]{1,2,0:T(1,128)S(1)}, u32[]{:S(2)}, u32[]{:S(2)}) %all-to-all-start) | async-done | bytes 800 | tf_op jit(solution)/shard_map/all_to_all | solution.py:207
  28.3 3.6 %slice_reduce_fusion.2 = (s32[64]{0:T(128)S(1)}, s32[64]{0:T(128)S(1)}, s32[64]{0:T(128)S(1)}) fusion(s32[64,3,1]{1,2,0:T(1,128)S(1)} %all-to-all-done), kind=kLoop, calls=%fused_computation.9 | loop fusion | bytes 1536 | tf_op jit(solution)/shard_map/slice | solution.py:220
  35.2 0.6 slice.147
  35.8 0.6 fusion.20
  39.4 0.6 fusion.19
  43.1 0.7 multiply_bitcast_fusion
  43.7 0.7 stack.17
  44.5 0.7 copy.47
  45.2 4.7 %all-to-all-start.1 = ((s32[64,1,5]{2,1,0:T(1,128)}), s32[64,1,5]{2,1,0:T(1,128)S(1)}, u32[]{:S(2)}, u32[]{:S(2)}) async-start(s32[64,1,5]{2,1,0:T(1,128)} %copy.47), calls=%async_computation.1 | async-start | bytes 65536 | tf_op jit(solution)/shard_map/all_to_all | solution.py:313
  49.9 1.1 fusion
  51.0 0.5 broadcast.127
  51.5 1.0 reduce.10
  52.5 1.2 %reshape.178 = bf16[64,2,2048]{2,1,0:T(2,128)(2,1)} reshape(bf16[64,4096]{1,0:T(8,128)(2,1)S(1)} %reduce.10) | data formatting | bytes 1048576
  53.7 5.7 %all-to-all-done.1 = s32[64,1,5]{2,1,0:T(1,128)S(1)} async-done(((s32[64,1,5]{2,1,0:T(1,128)}), s32[64,1,5]{2,1,0:T(1,128)S(1)}, u32[]{:S(2)}, u32[]{:S(2)}) %all-to-all-start.1) | async-done | bytes 1312 | tf_op jit(solution)/shard_map/all_to_all | solution.py:313
  59.4 4.7 %all-to-all-start.2 = ((bf16[64,2,2048]{2,1,0:T(2,128)(2,1)}), bf16[64,2,2048]{2,1,0:T(2,128)(2,1)S(1)}, u32[]{:S(2)}, u32[]{:S(2)}) async-start(bf16[64,2,2048]{2,1,0:T(2,128)(2,1)} %reshape.178), calls=%async_computation.2 | async-start | bytes 1048576 | tf_op jit(solution)/shard_map/all_to_all | solution.py:312
  64.1 1.4 %copy.51.extents = s32[32,2]{1,0:T(8,128)} copy(s32[32,2]{0,1:T(2,128)} %param.18) | data formatting | bytes 512 | tf_op args[4]
  65.6 0.2 slice_reduce_fusion
  65.8 0.2 fusion.3
  66.0 0.1 multiply_reduce_fusion
  66.2 0.7 copy.50.info
  66.9 15.1 %all-to-all-done.2 = bf16[64,2,2048]{2,1,0:T(2,128)(2,1)S(1)} async-done(((bf16[64,2,2048]{2,1,0:T(2,128)(2,1)}), bf16[64,2,2048]{2,1,0:T(2,128)(2,1)S(1)}, u32[]{:S(2)}, u32[]{:S(2)}) %all-to-all-start.2) | async-done | bytes 524320 | tf_op jit(solution)/shard_map/all_to_all | solution.py:312
  81.9 0.5 reshape.179
  82.5 0.7 convolution_convert_fusion.1
  83.1 10.6 %all_gather.3.xt = bf16[4,64,256]{2,1,0:T(8,128)(2,1)} all-gather(bf16[4,16,256]{2,1,0:T(8,128)(2,1)S(1)} %bitcast.41), channel_id=1, replica_groups=mesh['seq'=64,'head'=4] {'head'}, dimensions={1}, use_global_device_ids=true | all-gather | bytes 163840 | tf_op jit(solution)/shard_map/all_gather | solution.py:321
  93.7 17.3 %finish.1 = (bf16[1024,768]{1,0:T(8,128)(2,1)}, bf16[1024,768]{1,0:T(8,128)(2,1)}) custom-call(s32[4,3]{1,0:T(4,128)} %copy.50.info, s32[32,2]{1,0:T(8,128)} %copy.51.extents, bf16[4,64,256]{2,1,0:T(8,128)(2,1)} %all_gather.3.xt, bf16[64,3072]{1,0:T(8,128)(2,1)} %we.1, f32[1,3072]{1,0:T(1,128)} %bitcast.44, bf16[32,3072]{1,0:T(8,128)(2,1)} %shift.1, ...), custom_call_target="tpu_custom_call" | custom-call | tf_op jit(solution)/shard_map/finish/pallas_call | solution.py:182
  (47 shorter events, 3.4 us)
Async XLA Ops:
  0.6 20.0 %copy-start = (bf16[2,256,64]{1,2,0:T(8,128)(2,1)S(1)}, bf16[2,256,64]{1,2,0:T(8,128)(2,1)}, u32[]{:S(2)}) copy-start(bf16[2,256,64]{1,2,0:T(8,128)(2,1)} %param.14) | copy-start | bytes 196612
  5.9 22.5 %all-to-all-start = ((s32[64,3,1]{1,2,0:T(1,128)}), s32[64,3,1]{1,2,0:T(1,128)S(1)}, u32[]{:S(2)}, u32[]{:S(2)}) async-start(s32[64,3,1]{1,2,0:T(1,128)} %broadcast_in_dim.61), calls=%async_computation | async-start | bytes 65536 | tf_op jit(solution)/shard_map/all_to_all | solution.py:207
  45.2 14.1 %all-to-all-start.1 = ((s32[64,1,5]{2,1,0:T(1,128)}), s32[64,1,5]{2,1,0:T(1,128)S(1)}, u32[]{:S(2)}, u32[]{:S(2)}) async-start(s32[64,1,5]{2,1,0:T(1,128)} %copy.47), calls=%async_computation.1 | async-start | bytes 65536 | tf_op jit(solution)/shard_map/all_to_all | solution.py:313
  59.4 22.6 %all-to-all-start.2 = ((bf16[64,2,2048]{2,1,0:T(2,128)(2,1)}), bf16[64,2,2048]{2,1,0:T(2,128)(2,1)S(1)}, u32[]{:S(2)}, u32[]{:S(2)}) async-start(bf16[64,2,2048]{2,1,0:T(2,128)(2,1)} %reshape.178), calls=%async_computation.2 | async-start | bytes 1048576 | tf_op jit(solution)/shard_map/all_to_all | solution.py:312

commit v2 on v1

v2 whole, which is shorter than its diff:
```python
import functools
import jax
import jax.numpy as jnp
import numpy as np
from jax import lax
from jax.experimental import pallas as pl
from jax.experimental.pallas import tpu as pltpu
from jax.sharding import PartitionSpec as P

F32, BF16, I32 = jnp.float32, jnp.bfloat16, jnp.int32
HIGH = lax.Precision.HIGHEST
MESH = pl.DeviceIdType.MESH


def rope_table():
    table = np.zeros((128, 256), np.float32)
    row = lane = 0
    for places, width in ((32, 16), (48, 56), (48, 56)):
        rate = 1.0 / 10000.0 ** (np.arange(0, width, 2, dtype=np.float32) / np.float32(width))
        angle = np.arange(places, dtype=np.float32)[:, None] * rate[None, :].astype(np.float32)
        span = slice(lane, lane + width)
        table[row : row + places, span] = np.repeat(np.cos(angle), 2, axis=1)
        sines = np.repeat(np.sin(angle), 2, axis=1)
        sines[:, 0::2] *= -1.0
        table[row : row + places, 128 + lane : 128 + lane + width] = sines
        row, lane = row + places, lane + width
    return table


def lane_swapped(x):
    width = x.shape[-1]
    even = lax.broadcasted_iota(I32, x.shape, 1) % 2 == 0
    return jnp.where(even, pltpu.roll(x, width - 1, 1), pltpu.roll(x, 1, 1))


def halves(x):
    top = x.astype(BF16)
    return top, (x - top.astype(F32)).astype(BF16)


def finish_kernel(
    meta, extents, xt, we, be, shift, scale, gq, gk, table, wq, wk,
    oq, ok,
    w, left, shift_f, scale_f, zz, cs, eps, out, w_sem, o_sem,
):
    heads, slots, share, tokens = xt.shape
    channels, depth = we.shape
    chunks, _, wide = w.shape
    per = chunks // 2

    def weight_copy(n):
        source = (wq if n < per else wk).at[:, pl.ds((n % per) * wide, wide)]
        return pltpu.make_async_copy(source, w.at[n], w_sem.at[n])

    for n in range(chunks):
        weight_copy(n).start()

    me = lax.axis_index("seq")
    at_lane = lax.broadcasted_iota(I32, (8, 128), 1)
    code = me * slots + lax.broadcasted_iota(I32, (8, 128), 0)
    clip_row = jnp.broadcast_to(meta[0:1, :], (8, 128))
    found = jnp.broadcast_to(meta[1:2, :], (8, 128)) == code
    clip_at = jnp.sum(jnp.where(found, clip_row, 0), axis=1, keepdims=True)
    block_at = jnp.sum(jnp.where(found, at_lane, 0), axis=1, keepdims=True)
    used_at = jnp.sum(jnp.where(found, 1, 0), axis=1, keepdims=True)
    earlier = jnp.sum(jnp.where(clip_row < clip_at, 1, 0), axis=1, keepdims=True)
    offset_at = (block_at - earlier) * tokens
    clip_of = [clip_at[s, 0] for s in range(slots)]
    used_of = [used_at[s, 0] for s in range(slots)]
    offset_of = [offset_at[s, 0] for s in range(slots)]

    shift_f[...] = shift[...].astype(F32)
    scale_f[...] = scale[...].astype(F32)
    a = we[...].astype(F32)
    a = a - jnp.mean(a, axis=1, keepdims=True)
    b = be[...]
    b = b - jnp.mean(b, axis=1, keepdims=True)
    sub8 = lax.broadcasted_iota(I32, (8, depth), 0)
    b8 = jnp.where(sub8 == 0, b, 0.0)
    whole = jnp.concatenate([a, b8], axis=0)
    gram = lax.dot_general(
        whole, whole, (((1,), (1,)), ((), ())), precision=HIGH, preferred_element_type=F32
    ) * (1.0 / depth)

    extra = []
    for s in range(slots):
        clip = clip_of[s]
        gain = 1.0 + scale_f[pl.ds(clip, 1), :]
        left[pl.ds(s * channels, channels), :] = (a * gain).astype(BF16)
        move = shift_f[pl.ds(clip, 1), :]
        extra.append(jnp.where(sub8 == 0, b * gain, jnp.where(sub8 <= 2, move, 0.0)))
    left[pl.ds(slots * channels, 8 * slots), :] = jnp.concatenate(extra, axis=0).astype(BF16)

    lane = lax.broadcasted_iota(I32, (1, 128), 1)
    sub = lax.broadcasted_iota(I32, (8, tokens), 0)
    both = []
    for g in (gq, gk):
        gain = jnp.concatenate([g[...], lane_swapped(g[...])], axis=1)
        both.extend(halves(table[...] * gain))
    q_table = jnp.concatenate([both[0], both[1]], axis=0)
    k_table = jnp.concatenate([both[2], both[3]], axis=0)
    for s in range(slots):
        x = jnp.concatenate([xt[h, s] for h in range(heads)], axis=0).astype(F32)
        x1 = jnp.concatenate([x, jnp.where(sub == 0, 1.0, 0.0)], axis=0)
        y = jnp.dot(gram, x1, precision=HIGH, preferred_element_type=F32)
        var = jnp.maximum(jnp.sum(y * x1, axis=0, keepdims=True), 0.0) + 1e-06
        dev = jnp.sqrt(var)
        dev_hi = dev.astype(BF16).astype(F32)
        more = jnp.where(
            sub == 0, 1.0,
            jnp.where(sub == 1, dev_hi,
                      jnp.where(sub == 2, dev - dev_hi, jnp.where(sub == 3, var * 1e-06, 0.0))),
        )
        zt = jnp.concatenate([x, more, jnp.zeros((128 - channels - 8, tokens), F32)], axis=0)
        z = zt.T
        zb = z.astype(BF16)
        zz[pl.ds(s * tokens, tokens), :] = jnp.concatenate([zb, zb], axis=1)
        eps[s] = jnp.broadcast_to(z[:, channels + 3 : channels + 4], (tokens, 128))
        clip = clip_of[s]
        high = jnp.full((1, 128), extents[0, clip], I32).astype(F32)
        width = jnp.full((1, 128), extents[1, clip], I32).astype(F32)
        index = (offset_of[s] + lax.broadcasted_iota(I32, (tokens, 128), 0)).astype(F32)
        frame = jnp.floor((index + 0.5) * (1.0 / (high * width)))
        line = jnp.floor((index + 0.5) * (1.0 / width))
        place = jnp.where(
            lane < 32, frame, jnp.where(lane < 80, line - high * frame + 32.0, index - width * line + 80.0)
        )
        hot = jnp.where(place == lane.astype(F32), 1.0, 0.0).astype(BF16)
        hot = jnp.concatenate([hot, hot], axis=1)
        cs[0, s] = jnp.dot(hot, q_table, preferred_element_type=F32)
        cs[1, s] = jnp.dot(hot, k_table, preferred_element_type=F32)

    r_i = lax.broadcasted_iota(I32, (wide, wide), 0) // 128
    c_i = lax.broadcasted_iota(I32, (wide, wide), 1) // 128
    ones = jnp.where(r_i == c_i, 1.0, 0.0).astype(BF16)
    empty = jnp.zeros((128 - channels - 8, wide), F32)

    def out_copies(n):
        return (
            pltpu.make_async_copy(out.at[n], oq.at[:, pl.ds((n % per) * wide, wide)], o_sem.at[n]),
            pltpu.make_async_copy(out.at[n], ok.at[:, pl.ds((n % per) * wide, wide)], o_sem.at[n]),
        )

    def stack(m, s):
        own = jnp.concatenate(
            [m[s * channels : (s + 1) * channels],
             m[slots * channels + 8 * s : slots * channels + 8 * s + 8], empty], axis=0)
        hi, lo = halves(own)
        return jnp.concatenate([hi, lo], axis=0)

    def chunk(n, carry):
        which = n // per
        pltpu.make_async_copy(wq.at[:, pl.ds(0, wide)], w.at[n], w_sem.at[n]).wait()
        m = jnp.dot(left[...], w[n], preferred_element_type=F32)
        turned = lane_swapped(m)
        for s in range(slots):
            z = zz[pl.ds(s * tokens, tokens), :]
            v = jnp.dot(z, stack(m, s), preferred_element_type=F32)
            vs = jnp.dot(z, stack(turned, s), preferred_element_type=F32)
            power = jnp.dot((v * v).astype(BF16), ones, preferred_element_type=F32)
            c = cs[which, s, :, 0:128]
            sn = cs[which, s, :, 128:256]
            e = eps[s]
            for h in range(wide // 128):
                at = slice(h * 128, (h + 1) * 128)
                inverse = lax.rsqrt(power[:, at] * (1.0 / 128.0) + e)
                o = (v[:, at] * c + vs[:, at] * sn) * inverse
                o = jnp.where(used_of[s] > 0, o, 0.0)
                out[n, pl.ds(s * tokens, tokens), at] = o.astype(BF16)
        to_q, to_k = out_copies(n)

        @pl.when(n < per)
        def _():
            to_q.start()

        @pl.when(n >= per)
        def _():
            to_k.start()

        return carry

    lax.fori_loop(0, chunks, chunk, 0)
    for n in range(chunks):
        out_copies(n)[n // per].wait()


def finished(meta, extents, xt, we, be, shift, scale, gq, gk, wq, wk):
    heads, slots, share, tokens = xt.shape
    channels = heads * share
    clips, depth = shift.shape
    columns = wq.shape[1]
    wide = 256
    chunks = 2 * columns // wide
    rows = slots * tokens
    vmem = pl.BlockSpec(memory_space=pltpu.VMEM)
    smem = pl.BlockSpec(memory_space=pltpu.SMEM)
    hbm = pl.BlockSpec(memory_space=pl.ANY)
    return pl.pallas_call(
        finish_kernel,
        out_shape=[jax.ShapeDtypeStruct((rows, columns), BF16)] * 2,
        in_specs=[vmem, smem] + [vmem] * 8 + [hbm, hbm],
        out_specs=[hbm, hbm],
        scratch_shapes=[
            pltpu.VMEM((chunks, depth, wide), BF16),
            pltpu.VMEM((slots * (channels + 8), depth), BF16),
            pltpu.VMEM((clips, depth), F32),
            pltpu.VMEM((clips, depth), F32),
            pltpu.VMEM((rows, 256), BF16),
            pltpu.VMEM((2, slots, tokens, 256), F32),
            pltpu.VMEM((slots, tokens, 128), F32),
            pltpu.VMEM((chunks, rows, wide), BF16),
            pltpu.SemaphoreType.DMA((chunks,)),
            pltpu.SemaphoreType.DMA((chunks,)),
        ],
        compiler_params=pltpu.CompilerParams(vmem_limit_bytes=60 << 20),
        name="finish",
    )(meta, extents.T, xt, we, be.reshape(1, -1), shift, scale, gq.reshape(1, -1), gk.reshape(1, -1),
      jnp.asarray(rope_table()), wq, wk)


def routing_kernel(
    clips, owners, slot_ids, latents,
    xt, meta,
    near, tags, frame, wanted, side, side_tags,
    in_sem, s1, r1, t1, u1, s2, r2, t2, u2, s3, r3,
    *, deep, across,
):
    me = lax.axis_index("seq")
    x = lax.axis_index("head")
    heads = xt.shape[0]
    blocks, share, tokens = near.shape[1:]
    group = 2 * across
    plane, within = me // group, me % group
    y, core = within // 2, within % 2
    own = xt.shape[1]

    def z_peer(r):
        return {"seq": (plane + r) % deep * group + within}

    def y_peer(r):
        return {"seq": plane * group + (y + r // 2) % across * 2 + (core + r) % 2}

    def x_peer(r):
        return {"head": (x + r) % heads}

    z_steps = sorted(range(1, deep), key=lambda r: -min(r, deep - r))
    y_steps = sorted(range(1, group), key=lambda r: -min(r // 2, across - r // 2))
    x_steps = sorted(range(1, heads), key=lambda r: -min(r, heads - r))
    barrier = pltpu.get_barrier_semaphore()
    for peer in [z_peer(r) for r in z_steps] + [y_peer(r) for r in y_steps] + [x_peer(r) for r in x_steps]:
        pl.semaphore_signal(barrier, inc=1, device_id=peer, device_id_type=MESH)
    take = pltpu.make_async_copy(latents.at[:, pl.ds(x * share, share), :], near.at[0], in_sem)
    take.start()

    sub = lax.broadcasted_iota(I32, (8, 128), 0)
    lane = lax.broadcasted_iota(I32, (8, 128), 1)
    tag = jnp.zeros((8, 128), I32)
    for j in range(blocks):
        code = owners[j] * own + slot_ids[j]
        here = lane == blocks * me + j
        tag = tag + jnp.where(here & (sub == 0), clips[j], 0)
        tag = tag + jnp.where(here & (sub == 1), code, 0)
        tag = tag + jnp.where(sub == 2 + j, code, 0)
    tags[0] = tag
    for r in range(group):
        for s in range(own):
            code = y_peer(r)["seq"] * own + s
            wanted[r * own + s] = jnp.full((share, tokens), code, I32).astype(F32).astype(BF16)
    take.wait()
    pl.semaphore_wait(barrier, deep + group + heads - 3)

    def z_copies(r):
        return (
            pltpu.make_async_remote_copy(
                near.at[0], near.at[r], s1.at[r], r1.at[r], device_id=z_peer(r), device_id_type=MESH),
            pltpu.make_async_remote_copy(
                tags.at[0], tags.at[r], t1.at[r], u1.at[r], device_id=z_peer(r), device_id_type=MESH),
        )

    sent = []
    for r in z_steps:
        data, words = z_copies(r)
        data.start()
        words.start()
        sent += [data, words]

    def sort_in(r, first):
        for j in range(blocks):
            code = jnp.broadcast_to(tags[r, 2 + j : 3 + j, :], (share, 128)).astype(F32).astype(BF16)
            code = jnp.concatenate([code] * (tokens // 128), axis=1)
            hit = wanted[...] == code[None]
            before = jnp.zeros(frame.shape, BF16) if first and j == 0 else frame[...]
            frame[...] = jnp.where(hit, near[r, j][None], before)

    sort_in(0, True)
    total = tags[0]
    for r in reversed(z_steps):
        data, words = z_copies(r)
        data.wait_recv()
        words.wait_recv()
        sort_in(r, False)
        total = total + tags[r]
    side_tags[0] = total

    def y_copies(r):
        return (
            pltpu.make_async_remote_copy(
                frame.at[pl.ds(r * own, own)], side.at[r], s2.at[r], r2.at[r],
                device_id=y_peer(r), device_id_type=MESH),
            pltpu.make_async_remote_copy(
                side_tags.at[0], side_tags.at[r], t2.at[r], u2.at[r],
                device_id=y_peer(r), device_id_type=MESH),
        )

    for r in y_steps:
        data, words = y_copies(r)
        data.start()
        words.start()
        sent += [data, words]
    mine = frame[0:own]
    for r in reversed(y_steps):
        data, words = y_copies(r)
        data.wait_recv()
        words.wait_recv()
        mine = mine + side[r]
        total = total + side_tags[r]
    xt[x] = mine

    def x_copy(r):
        return pltpu.make_async_remote_copy(
            xt.at[x], xt.at[x], s3.at[r], r3.at[r], device_id=x_peer(r), device_id_type=MESH)

    for r in x_steps:
        copy = x_copy(r)
        copy.start()
        sent.append(copy)
    meta[...] = total
    for r in reversed(x_steps):
        at = xt.at[(x + heads - r) % heads]
        pltpu.make_async_remote_copy(
            at, at, s3.at[r], r3.at[r], device_id=x_peer(r), device_id_type=MESH).wait_recv()
    for copy in sent:
        copy.wait_send()


def routed(clips, owners, slot_ids, latents, own, heads, deep, across):
    blocks, channels, tokens = latents.shape
    share = channels // heads
    group = 2 * across
    vmem = pl.BlockSpec(memory_space=pltpu.VMEM)
    smem = pl.BlockSpec(memory_space=pltpu.SMEM)
    hbm = pl.BlockSpec(memory_space=pl.ANY)
    dma = pltpu.SemaphoreType.DMA
    return pl.pallas_call(
        functools.partial(routing_kernel, deep=deep, across=across),
        out_shape=[
            jax.ShapeDtypeStruct((heads, own, share, tokens), BF16),
            jax.ShapeDtypeStruct((8, 128), I32),
        ],
        in_specs=[smem, smem, smem, hbm],
        out_specs=[vmem, vmem],
        scratch_shapes=[
            pltpu.VMEM((deep, blocks, share, tokens), BF16),
            pltpu.VMEM((deep, 8, 128), I32),
            pltpu.VMEM((group * own, share, tokens), BF16),
            pltpu.VMEM((group * own, share, tokens), BF16),
            pltpu.VMEM((group, own, share, tokens), BF16),
            pltpu.VMEM((group, 8, 128), I32),
            dma,
            dma((deep,)), dma((deep,)), dma((deep,)), dma((deep,)),
            dma((group,)), dma((group,)), dma((group,)), dma((group,)),
            dma((heads,)), dma((heads,)),
        ],
        compiler_params=pltpu.CompilerParams(
            collective_id=0, has_side_effects=True, vmem_limit_bytes=16 << 20),
        name="routing",
    )(clips, owners, slot_ids, latents)


def per_device(
    across, latents, clip_ids, owners, slots, extents, embed_weight, embed_bias, shift_table, scale_table,
    query_weight, key_weight, query_gain, key_gain,
):
    local = latents.shape[0]
    own = 2 * local
    heads, ranks = lax.axis_size("head"), lax.axis_size("seq")
    xt, meta = routed(
        clip_ids, owners, slots, jnp.transpose(latents, (0, 2, 1)), own, heads, ranks // (2 * across), across
    )
    return tuple(
        finished(
            meta, extents, xt, embed_weight, embed_bias, shift_table, scale_table,
            query_gain, key_gain, query_weight, key_weight,
        )
    )


def solution(mesh):
    placed = (
        P("seq", None, None),
        P("seq"),
        P("seq"),
        P("seq"),
        P(),
        P(),
        P(),
        P(),
        P(),
        P(None, "head"),
        P(None, "head"),
        P(),
        P(),
    )
    return jax.shard_map(
        functools.partial(per_device, 4),
        mesh=mesh,
        in_specs=placed,
        out_specs=(P("seq", "head"), P("seq", "head")),
        check_vma=False,
    )
```

time: 113 us -> 46.9 us (0.42); the launches traced: 111 us -> 46.7 us
  waiting for transfers between devices: 28.4 us -> 0 us
  Pallas kernels: 17.3 us -> 42 us
  starting transfers between devices: 22.6 us -> 0 us
  local copies, waits for them, and re-layouts: 16.4 us -> 4.03 us
  blocking collectives: 10.6 us -> 0 us
  other arithmetic: 7.09 us -> 0 us
  between operations: 7.08 us -> 0.66 us
  matrix products: 1.74 us -> 0 us
    all_to_all x3 -> x0, waiting for transfers between devices: 28.4 us -> none  [the longest x1 15.1 us: per_device(): lax.all_to_all(send_rows, 'seq', split_axis=0, concat_axis=0, tiled=True)]
    pallas_call x0 -> x1, Pallas kernels: none -> 24.9 us  [routed(): pl.pallas_call(functools.partial(routing_kernel, deep=deep, across=across...]
    all_to_all x3 -> x0, starting transfers between devices: 22.6 us -> none  [the longest x1 13.1 us: copy_for_each(): lax.all_to_all(jnp.broadcast_to(x[None], (length, *x.shape)), axis, 0, 0,...]
    all_gather x1 -> x0, blocking collectives: 10.6 us -> none  [per_device(): slot_latent = lax.all_gather(slot_latent, 'head', axis=1, tiled=True)]
    slice x38 -> x0, local copies, waits for them, and re-layouts: 10.1 us -> none  [the longest x33 4.83 us: combined_pairwise(): part[side::2]]
    reduce_sum x4 -> x0, other arithmetic: 3.09 us -> none  [the longest x1 1.94 us: per_device(): jnp.sum((clip_ids == final_clip[0]).astype(jnp.int32)).reshape(1)]
    dot_general x2 -> x0, matrix products: 1.74 us -> none  [the longest x1 1.07 us: per_device(): jnp.dot(target.T.astype(jnp.bfloat16), flat_rows, preferred_element_type=...]
    broadcast_in_dim x1 -> x0, other arithmetic: 1.37 us -> none  [copy_for_each(): jnp.broadcast_to(x[None], (length, *x.shape))]
  transfers between devices with their start and end apart: 3 -> 0, of which waited for: 3 -> 0; matrix products, arithmetic and copies ran while one was open for 7% -> 0% of each run, Pallas kernels for 0% -> 0%
where the time goes in v2:
time: 46.9 us; the launch traced here: 46.7 us
  Pallas kernels  42 us (90%)
  local copies, waits for them, and re-layouts  4.03 us (9%)
  between operations  0.66 us (1%)
    pallas_call x1, Pallas kernels, routed(): pl.pallas_call(functools.partial(routing_kernel, deep=deep, across=across...  24.9 us
    pallas_call x1, Pallas kernels, finished(): pl.pallas_call(finish_kernel, out_shape=[jax.ShapeDtypeStruct((rows, colu...  17.2 us
    unnamed x12, local copies, waits for them, and re-layouts  4.03 us

profile of v2, /device:TPU:1, one launch (start us, length us, event | category | flops | bytes accessed | tf_op | source)
XLA Modules:
  0.0 46.7 jit_solution(12153843588117618737)
XLA Ops:
  0.6 0.0 copy-start.1
  0.6 0.8 %copy-done.1 = bf16[2,256,64]{1,2,0:T(8,128)(2,1)S(1)} copy-done((bf16[2,256,64]{1,2,0:T(8,128)(2,1)S(1)}, bf16[2,256,64]{1,2,0:T(8,128)(2,1)}, u32[]{:S(2)}) %copy-start.1) | copy-done | bytes 65560
  1.5 0.0 copy-start.3
  1.5 0.7 %copy-done.3 = s32[2]{0:T(128)S(1)} copy-done((s32[2]{0:T(128)S(1)}, s32[2]{0:T(128)}, u32[]{:S(2)}) %copy-start.3) | copy-done | bytes 32
  2.1 0.0 copy-start.4
  2.1 0.7 %copy-done.4 = s32[2]{0:T(128)S(1)} copy-done((s32[2]{0:T(128)S(1)}, s32[2]{0:T(128)}, u32[]{:S(2)}) %copy-start.4) | copy-done | bytes 32
  2.8 0.0 copy-start.5
  2.8 0.7 %copy-done.5 = s32[2]{0:T(128)S(1)} copy-done((s32[2]{0:T(128)S(1)}, s32[2]{0:T(128)}, u32[]{:S(2)}) %copy-start.5) | copy-done | bytes 32
  3.4 24.9 %routing.1 = (bf16[4,4,16,256]{3,2,1,0:T(8,128)(2,1)S(1)}, s32[8,128]{1,0:T(8,128)S(1)}) custom-call(s32[2]{0:T(128)S(1)} %copy-done.3, s32[2]{0:T(128)S(1)} %copy-done.4, s32[2]{0:T(128)S(1)} %copy-done.5, bf16[2,64,256]{2,1,0:T(8,128)(2,1)S(1)} %bitcast.5), custom_call_target="tpu_custom_call" | custom-call | tf_op jit(solution)/shard_map/routing/pallas_call | solution.py:354
  28.3 0.0 copy-start
  28.3 0.6 %copy-done = bf16[4,4,16,256]{3,2,1,0:T(8,128)(2,1)} copy-done((bf16[4,4,16,256]{3,2,1,0:T(8,128)(2,1)}, bf16[4,4,16,256]{3,2,1,0:T(8,128)(2,1)S(1)}, u32[]{:S(2)}) %copy-start) | copy-done | bytes 131096
  29.0 0.0 copy-start.2
  29.0 0.6 %copy-done.2 = s32[8,128]{1,0:T(8,128)} copy-done((s32[8,128]{1,0:T(8,128)}, s32[8,128]{1,0:T(8,128)S(1)}, u32[]{:S(2)}) %copy-start.2) | copy-done | bytes 4120
  29.6 17.2 %finish.1 = (bf16[1024,768]{1,0:T(8,128)(2,1)}, bf16[1024,768]{1,0:T(8,128)(2,1)}) custom-call(s32[8,128]{1,0:T(8,128)} %copy-done.2, s32[2,32]{1,0:T(2,128)} %bitcast.7, bf16[4,4,16,256]{3,2,1,0:T(8,128)(2,1)} %copy-done, bf16[64,3072]{1,0:T(8,128)(2,1)} %we.1, f32[1,3072]{1,0:T(1,128)} %bitcast.6, bf16[32,3072]{1,0:T(8,128)(2,1)} %shift.1, ...), custom_call_target="tpu_custom_call" | custom-call | tf_op jit(solution)/shard_map/finish/pallas_call | solution.py:198
Async XLA Ops:
  0.6 0.8 %copy-start.1 = (bf16[2,256,64]{1,2,0:T(8,128)(2,1)S(1)}, bf16[2,256,64]{1,2,0:T(8,128)(2,1)}, u32[]{:S(2)}) copy-start(bf16[2,256,64]{1,2,0:T(8,128)(2,1)} %param.14) | copy-start | bytes 196612
  1.5 0.7 %copy-start.3 = (s32[2]{0:T(128)S(1)}, s32[2]{0:T(128)}, u32[]{:S(2)}) copy-start(s32[2]{0:T(128)} %clips.1) | copy-start | bytes 28
  2.1 0.7 %copy-start.4 = (s32[2]{0:T(128)S(1)}, s32[2]{0:T(128)}, u32[]{:S(2)}) copy-start(s32[2]{0:T(128)} %owners.1) | copy-start | bytes 28
  2.8 0.7 %copy-start.5 = (s32[2]{0:T(128)S(1)}, s32[2]{0:T(128)}, u32[]{:S(2)}) copy-start(s32[2]{0:T(128)} %slot_ids.1) | copy-start | bytes 28
  28.3 0.6 %copy-start = (bf16[4,4,16,256]{3,2,1,0:T(8,128)(2,1)}, bf16[4,4,16,256]{3,2,1,0:T(8,128)(2,1)S(1)}, u32[]{:S(2)}) copy-start(bf16[4,4,16,256]{3,2,1,0:T(8,128)(2,1)S(1)} %get-tuple-element.5.xt) | copy-start | bytes 393220
  29.0 0.6 %copy-start.2 = (s32[8,128]{1,0:T(8,128)}, s32[8,128]{1,0:T(8,128)S(1)}, u32[]{:S(2)}) copy-start(s32[8,128]{1,0:T(8,128)S(1)} %get-tuple-element.4.meta) | copy-start | bytes 12292

commit v3 on v2

v3 whole, which is shorter than its diff:
```python
import functools
import jax
import jax.numpy as jnp
import numpy as np
from jax import lax
from jax.experimental import pallas as pl
from jax.experimental.pallas import tpu as pltpu
from jax.sharding import PartitionSpec as P

F32, BF16, I32 = jnp.float32, jnp.bfloat16, jnp.int32
HIGH = lax.Precision.HIGHEST
MESH = pl.DeviceIdType.MESH
WIDE = 256
HBM = pl.BlockSpec(memory_space=pltpu.HBM)
VMEM = pl.BlockSpec(memory_space=pltpu.VMEM)


def rope_table():
    table = np.zeros((128, 256), np.float32)
    row = lane = 0
    for places, width in ((32, 16), (48, 56), (48, 56)):
        rate = 1.0 / 10000.0 ** (np.arange(0, width, 2, dtype=np.float32) / np.float32(width))
        angle = np.arange(places, dtype=np.float32)[:, None] * rate[None, :].astype(np.float32)
        span = slice(lane, lane + width)
        table[row : row + places, span] = np.repeat(np.cos(angle), 2, axis=1)
        sines = np.repeat(np.sin(angle), 2, axis=1)
        sines[:, 0::2] *= -1.0
        table[row : row + places, 128 + lane : 128 + lane + width] = sines
        row, lane = row + places, lane + width
    return table


def lane_swapped(x):
    width = x.shape[-1]
    even = lax.broadcasted_iota(I32, x.shape, 1) % 2 == 0
    return jnp.where(even, pltpu.roll(x, width - 1, 1), pltpu.roll(x, 1, 1))


def halves(x):
    top = x.astype(BF16)
    return top, (x - top.astype(F32)).astype(BF16)


def routing_kernel(
    clips_h, owners_h, slots_h, latents, extents_h, we_h, be_h, shift_h, scale_h, gq_h, gk_h, table_h, wq, wk,
    xt, m_out, cs, gram_out, use,
    clips, owners, slot_ids, extents, we, be, shift, scale, gq, gk, table, w, left, base, halved,
    near, tags, frame, wanted, side, side_tags,
    in_sem, w_sem, s1, r1, t1, u1, s2, r2, t2, u2, s3, r3,
    *, deep, across,
):
    me = lax.axis_index("seq")
    x = lax.axis_index("head")
    heads = xt.shape[0]
    blocks, share, tokens = near.shape[1:]
    group = 2 * across
    plane, within = me // group, me % group
    y, core = within // 2, within % 2
    own = xt.shape[1]
    channels, depth = we_h.shape
    per = w.shape[0] // 2

    def z_peer(r):
        return {"seq": (plane + r) % deep * group + within}

    def y_peer(r):
        return {"seq": plane * group + (y + r // 2) % across * 2 + (core + r) % 2}

    def x_peer(r):
        return {"head": (x + r) % heads}

    z_steps = sorted(range(1, deep), key=lambda r: -min(r, deep - r))
    y_steps = sorted(range(1, group), key=lambda r: -min(r // 2, across - r // 2))
    x_steps = sorted(range(1, heads), key=lambda r: -min(r, heads - r))
    barrier = pltpu.get_barrier_semaphore()
    for peer in [z_peer(r) for r in z_steps] + [y_peer(r) for r in y_steps] + [x_peer(r) for r in x_steps]:
        pl.semaphore_signal(barrier, inc=1, device_id=peer, device_id_type=MESH)

    takes = [
        pltpu.make_async_copy(source, place, in_sem.at[k])
        for k, (source, place) in enumerate((
            (clips_h, clips), (owners_h, owners), (slots_h, slot_ids),
            (latents.at[:, pl.ds(x * share, share), :], near.at[0]),
            (we_h, we), (be_h, be), (gq_h, gq), (gk_h, gk), (table_h, table),
            (shift_h, shift), (scale_h, scale), (extents_h, extents),
        ))
    ]
    weights = [
        pltpu.make_async_copy(source.at[:, pl.ds(n * WIDE, WIDE)], w.at[k * per + n], w_sem.at[k * per + n])
        for n in range(per) for k, source in enumerate((wq, wk))
    ]
    for copy in takes + weights:
        copy.start()

    sub = lax.broadcasted_iota(I32, (8, 128), 0)
    lane = lax.broadcasted_iota(I32, (8, 128), 1)
    for r in range(group):
        for s in range(own):
            code = y_peer(r)["seq"] * own + s
            wanted[r * own + s] = jnp.full((share, tokens), code, I32).astype(F32).astype(BF16)
    for copy in takes[:3]:
        copy.wait()
    tag = jnp.zeros((8, 128), I32)
    for j in range(blocks):
        code = owners[j] * own + slot_ids[j]
        here = lane == blocks * me + j
        tag = tag + jnp.where(here & (sub == 0), clips[j], 0)
        tag = tag + jnp.where(here & (sub == 1), code, 0)
        tag = tag + jnp.where(sub == 2 + j, code, 0)
    tags[0] = tag
    takes[3].wait()
    pl.semaphore_wait(barrier, deep + group + heads - 3)

    def z_copies(r):
        return (
            pltpu.make_async_remote_copy(
                near.at[0], near.at[r], s1.at[r], r1.at[r], device_id=z_peer(r), device_id_type=MESH),
            pltpu.make_async_remote_copy(
                tags.at[0], tags.at[r], t1.at[r], u1.at[r], device_id=z_peer(r), device_id_type=MESH),
        )

    sent = []
    for r in z_steps:
        data, words = z_copies(r)
        data.start()
        words.start()
        sent += [data, words]

    def sort_in(r, first):
        for j in range(blocks):
            code = jnp.broadcast_to(tags[r, 2 + j : 3 + j, :], (share, 128)).astype(F32).astype(BF16)
            code = jnp.concatenate([code] * (tokens // 128), axis=1)
            hit = wanted[...] == code[None]
            before = jnp.zeros(frame.shape, BF16) if first and j == 0 else frame[...]
            frame[...] = jnp.where(hit, near[r, j][None], before)

    for copy in takes[4:]:
        copy.wait()
    a = we[...].astype(F32)
    a = a - jnp.mean(a, axis=1, keepdims=True)
    b = be[...]
    b = b - jnp.mean(b, axis=1, keepdims=True)
    sub16 = lax.broadcasted_iota(I32, (16, depth), 0)
    base[0:channels, :] = a
    base[channels : channels + 16, :] = jnp.where(sub16 == 0, b, 0.0)
    gram = lax.dot_general(
        base[...], base[...], (((1,), (1,)), ((), ())), precision=HIGH, preferred_element_type=F32
    ) * (1.0 / depth)
    for k in range(3):
        part = gram.astype(BF16)
        gram_out[k] = part
        gram = gram - part.astype(F32)
    for k, g in enumerate((gq, gk)):
        gain = jnp.concatenate([g[...], lane_swapped(g[...])], axis=1)
        hi, lo = halves(table[...] * gain)
        halved[k, 0:128, :] = hi
        halved[k, 128:256, :] = lo

    sort_in(0, True)
    total = tags[0]
    for r in reversed(z_steps):
        data, words = z_copies(r)
        data.wait_recv()
        words.wait_recv()
        sort_in(r, False)
        total = total + tags[r]
    side_tags[0] = total

    def y_copies(r):
        return (
            pltpu.make_async_remote_copy(
                frame.at[pl.ds(r * own, own)], side.at[r], s2.at[r], r2.at[r],
                device_id=y_peer(r), device_id_type=MESH),
            pltpu.make_async_remote_copy(
                side_tags.at[0], side_tags.at[r], t2.at[r], u2.at[r],
                device_id=y_peer(r), device_id_type=MESH),
        )

    for r in y_steps:
        data, words = y_copies(r)
        words.start()
        data.start()
        sent += [data, words]
    mine = frame[0:own]
    for r in reversed(y_steps):
        data, words = y_copies(r)
        data.wait_recv()
        words.wait_recv()
        mine = mine + side[r]
        total = total + side_tags[r]
    xt[x] = mine

    def x_copy(r):
        return pltpu.make_async_remote_copy(
            xt.at[x], xt.at[x], s3.at[r], r3.at[r], device_id=x_peer(r), device_id_type=MESH)

    for r in x_steps:
        copy = x_copy(r)
        copy.start()
        sent.append(copy)

    clip_row = jnp.broadcast_to(total[0:1, :], (8, 128))
    found = jnp.broadcast_to(total[1:2, :], (8, 128)) == me * own + sub
    clip_at = jnp.sum(jnp.where(found, clip_row, 0), axis=1, keepdims=True)
    block_at = jnp.sum(jnp.where(found, lane, 0), axis=1, keepdims=True)
    used_at = jnp.sum(jnp.where(found, 1, 0), axis=1, keepdims=True)
    earlier = jnp.sum(jnp.where(clip_row < clip_at, 1, 0), axis=1, keepdims=True)
    offset_at = (block_at - earlier) * tokens
    use[...] = jnp.broadcast_to(used_at.astype(F32), (8, 128))
    count = shift.shape[0]
    among = lax.broadcasted_iota(I32, (8, count), 1) == clip_at
    high_at = jnp.sum(jnp.where(among, extents[0:1, :], 0), axis=1, keepdims=True).astype(F32)
    wide_at = jnp.sum(jnp.where(among, extents[1:2, :], 0), axis=1, keepdims=True).astype(F32)
    pick = jnp.where(among, 1.0, 0.0).astype(BF16)
    moves = jnp.dot(pick, shift[...], preferred_element_type=F32)
    gains = 1.0 + jnp.dot(pick, scale[...], preferred_element_type=F32)
    sub8 = lax.broadcasted_iota(I32, (8, depth), 0)
    extra = []
    for s in range(own):
        gain = gains[s : s + 1, :]
        left[s * channels : (s + 1) * channels, :] = (base[0:channels, :] * gain).astype(BF16)
        middle = base[channels : channels + 1, :] * gain
        extra.append(jnp.where(sub8 == 0, middle, jnp.where(sub8 <= 2, moves[s : s + 1, :], 0.0)))
    left[own * channels :, :] = jnp.concatenate(extra, axis=0).astype(BF16)
    for copy in weights:
        copy.wait()

    def project(n, carry):
        m_out[n] = jnp.dot(left[...], w[n], preferred_element_type=F32)
        m_out[n + per] = jnp.dot(left[...], w[n + per], preferred_element_type=F32)
        return carry

    lax.fori_loop(0, per, project, 0)

    lane_f = lax.broadcasted_iota(I32, (1, 128), 1).astype(F32)
    steps = lax.broadcasted_iota(I32, (tokens, 128), 0).astype(F32)
    for s in range(own):
        high, wide = high_at[s : s + 1, :], wide_at[s : s + 1, :]
        high, wide = jnp.maximum(high, 1.0), jnp.maximum(wide, 1.0)
        index = offset_at[s : s + 1, :].astype(F32) + steps
        frames = jnp.floor((index + 0.5) * (1.0 / (high * wide)))
        lines = jnp.floor((index + 0.5) * (1.0 / wide))
        place = jnp.where(
            lane_f < 32.0, frames,
            jnp.where(lane_f < 80.0, lines - high * frames + 32.0, index - wide * lines + 80.0),
        )
        hot = jnp.where(place == lane_f, 1.0, 0.0).astype(BF16)
        hot = jnp.concatenate([hot, hot], axis=1)
        cs[0, s] = jnp.dot(hot, halved[0], preferred_element_type=F32)
        cs[1, s] = jnp.dot(hot, halved[1], preferred_element_type=F32)

    for r in reversed(x_steps):
        at = xt.at[(x + heads - r) % heads]
        pltpu.make_async_remote_copy(
            at, at, s3.at[r], r3.at[r], device_id=x_peer(r), device_id_type=MESH).wait_recv()
    for copy in sent:
        copy.wait_send()


def routed(
    across, clips, owners, slot_ids, latents, extents, we, be, shift, scale, gq, gk, wq, wk
):
    blocks, channels, tokens = latents.shape
    own = 2 * blocks
    heads, deep = lax.axis_size("head"), lax.axis_size("seq") // (2 * across)
    share = channels // heads
    group = 2 * across
    depth, columns = wq.shape
    chunks = 2 * columns // WIDE
    dma, room = pltpu.SemaphoreType.DMA, pltpu.VMEM
    table = jnp.asarray(rope_table())
    flat = [v.reshape(1, -1) for v in (be, gq, gk)]
    rows = own * (channels + 8)
    args = (clips, owners, slot_ids, latents, extents.T, we, flat[0], shift, scale, flat[1], flat[2], table, wq, wk)
    return pl.pallas_call(
        functools.partial(routing_kernel, deep=deep, across=across),
        out_shape=[
            jax.ShapeDtypeStruct((heads, own, share, tokens), BF16),
            jax.ShapeDtypeStruct((chunks, rows, WIDE), F32),
            jax.ShapeDtypeStruct((2, own, tokens, 256), F32),
            jax.ShapeDtypeStruct((3, channels + 16, channels + 16), BF16),
            jax.ShapeDtypeStruct((8, 128), F32),
        ],
        in_specs=[HBM] * len(args),
        out_specs=[VMEM] * 5,
        scratch_shapes=[
            pltpu.SMEM(clips.shape, I32), pltpu.SMEM(clips.shape, I32), pltpu.SMEM(clips.shape, I32),
            *(room(v.shape, v.dtype) for v in (args[4], we, flat[0], shift, scale, flat[1], flat[2], table)),
            room((chunks, depth, WIDE), BF16),
            room((rows, depth), BF16),
            room((channels + 16, depth), F32),
            room((2, 256, 256), BF16),
            room((deep, blocks, share, tokens), BF16),
            room((deep, 8, 128), I32),
            room((group * own, share, tokens), BF16),
            room((group * own, share, tokens), BF16),
            room((group, own, share, tokens), BF16),
            room((group, 8, 128), I32),
            dma((12,)), dma((chunks,)),
            dma((deep,)), dma((deep,)), dma((deep,)), dma((deep,)),
            dma((group,)), dma((group,)), dma((group,)), dma((group,)),
            dma((heads,)), dma((heads,)),
        ],
        compiler_params=pltpu.CompilerParams(
            collective_id=0, has_side_effects=True, vmem_limit_bytes=28 << 20),
        name="routing",
    )(*(pltpu.with_memory_space_constraint(v, pltpu.HBM) for v in args))


def finish_kernel(xt, m_in, cs, gram, use, oq, ok, zz, eps, out, o_sem):
    heads, slots, share, tokens = xt.shape
    channels = heads * share
    chunks, _, wide = m_in.shape
    per = chunks // 2
    sub = lax.broadcasted_iota(I32, (16, tokens), 0)
    for s in range(slots):
        x = jnp.concatenate([xt[h, s] for h in range(heads)], axis=0)
        x1 = jnp.concatenate([x, jnp.where(sub == 0, 1.0, 0.0).astype(BF16)], axis=0)
        y = sum(jnp.dot(gram[k], x1, preferred_element_type=F32) for k in range(3))
        xf = x1.astype(F32)
        var = jnp.maximum(jnp.sum(y * xf, axis=0, keepdims=True), 0.0) + 1e-06
        dev = jnp.sqrt(var)
        dev_hi = dev.astype(BF16).astype(F32)
        more = jnp.where(
            sub == 0, 1.0,
            jnp.where(sub == 1, dev_hi,
                      jnp.where(sub == 2, dev - dev_hi, jnp.where(sub == 3, var * 1e-06, 0.0))),
        )
        zt = jnp.concatenate([xf[0:channels], more, jnp.zeros((112 - channels, tokens), F32)], axis=0)
        z = zt.T
        eps[s] = jnp.broadcast_to(z[:, channels + 3 : channels + 4], (tokens, 128))
        zb = (z * use[s : s + 1, :]).astype(BF16)
        zz[s] = jnp.concatenate([zb, zb], axis=1)

    r_i = lax.broadcasted_iota(I32, (wide, wide), 0) // 128
    c_i = lax.broadcasted_iota(I32, (wide, wide), 1) // 128
    ones = jnp.where(r_i == c_i, 1.0 / 128.0, 0.0).astype(BF16)
    empty = jnp.zeros((128 - channels - 8, wide), F32)

    def stack(m, s):
        own = jnp.concatenate(
            [m[s * channels : (s + 1) * channels],
             m[slots * channels + 8 * s : slots * channels + 8 * s + 8], empty], axis=0)
        hi, lo = halves(own)
        return jnp.concatenate([hi, lo], axis=0)

    def out_copy(n, place):
        return pltpu.make_async_copy(
            out.at[n], place.at[:, pl.ds(n % per * wide, wide)], o_sem.at[n])

    def chunk(n, carry):
        which = n // per
        m = m_in[n]
        turned = lane_swapped(m)
        for s in range(slots):
            z = zz[s]
            v = jnp.dot(z, stack(m, s), preferred_element_type=F32)
            vs = jnp.dot(z, stack(turned, s), preferred_element_type=F32)
            power = jnp.dot((v * v).astype(BF16), ones, preferred_element_type=F32)
            c = cs[which, s, :, 0:128]
            sn = cs[which, s, :, 128:256]
            e = eps[s]
            for h in range(wide // 128):
                at = slice(h * 128, (h + 1) * 128)
                o = (v[:, at] * c + vs[:, at] * sn) * lax.rsqrt(power[:, at] + e)
                out[n, s * tokens : (s + 1) * tokens, at] = o.astype(BF16)

        @pl.when(n < per)
        def _():
            out_copy(n, oq).start()

        @pl.when(n >= per)
        def _():
            out_copy(n, ok).start()

        return carry

    lax.fori_loop(0, chunks, chunk, 0)
    for n in range(chunks):
        out_copy(n, oq if n < per else ok).wait()


def finished(xt, m, cs, gram, use):
    heads, slots, share, tokens = xt.shape
    chunks, _, wide = m.shape
    rows = slots * tokens
    return pl.pallas_call(
        finish_kernel,
        out_shape=[jax.ShapeDtypeStruct((rows, chunks // 2 * wide), BF16)] * 2,
        in_specs=[VMEM] * 5,
        out_specs=[pl.BlockSpec(memory_space=pl.ANY)] * 2,
        scratch_shapes=[
            pltpu.VMEM((slots, tokens, 256), BF16),
            pltpu.VMEM((slots, tokens, 128), F32),
            pltpu.VMEM((chunks, rows, wide), BF16),
            pltpu.SemaphoreType.DMA((chunks,)),
        ],
        compiler_params=pltpu.CompilerParams(vmem_limit_bytes=28 << 20),
        name="finish",
    )(xt, m, cs, gram, use)


def per_device(
    across, latents, clip_ids, owners, slots, extents, embed_weight, embed_bias, shift_table, scale_table,
    query_weight, key_weight, query_gain, key_gain,
):
    parts = routed(
        across, clip_ids, owners, slots, jnp.transpose(latents, (0, 2, 1)), extents, embed_weight, embed_bias,
        shift_table, scale_table, query_gain, key_gain, query_weight, key_weight,
    )
    return tuple(finished(*parts))


def solution(mesh):
    placed = (
        P("seq", None, None),
        P("seq"),
        P("seq"),
        P("seq"),
        P(),
        P(),
        P(),
        P(),
        P(),
        P(None, "head"),
        P(None, "head"),
        P(),
        P(),
    )
    return jax.shard_map(
        functools.partial(per_device, 4),
        mesh=mesh,
        in_specs=placed,
        out_specs=(P("seq", "head"), P("seq", "head")),
        check_vma=False,
    )
```

time: 46.9 us -> 32.6 us (0.70)
  Pallas kernels: 42 us -> 31.9 us
  local copies, waits for them, and re-layouts: 4.03 us -> 0 us
    pallas_call x1, Pallas kernels: 17.2 us -> 6.22 us  [finished(): pl.pallas_call(finish_kernel, out_shape=[jax.ShapeDtypeStruct((rows, chun...]
    unnamed x12 -> x0, local copies, waits for them, and re-layouts: 4.03 us -> none
    pallas_call x1, Pallas kernels: 24.9 us -> 25.7 us  [routed(): pl.pallas_call(functools.partial(routing_kernel, deep=deep, across=across...]
where the time goes in v3:
time: 32.6 us; the launch traced here: 32.5 us
  Pallas kernels  31.9 us (98%)
  between operations  0.64 us (2%)
    pallas_call x1, Pallas kernels, routed(): pl.pallas_call(functools.partial(routing_kernel, deep=deep, across=across...  25.7 us
    pallas_call x1, Pallas kernels, finished(): pl.pallas_call(finish_kernel, out_shape=[jax.ShapeDtypeStruct((rows, chun...  6.22 us

profile of v3, /device:TPU:1, one launch (start us, length us, event | category | flops | bytes accessed | tf_op | source)
XLA Modules:
  0.0 32.5 jit_solution(2437117150754242984)
XLA Ops:
  0.6 25.7 %routing.1 = (bf16[4,4,16,256]{3,2,1,0:T(8,128)(2,1)S(1)}, f32[6,288,256]{2,1,0:T(8,128)S(1)}, f32[2,4,256,256]{3,2,1,0:T(8,128)S(1)}, bf16[3,80,80]{2,1,0:T(8,128)(2,1)S(1)}, f32[8,128]{1,0:T(8,128)S(1)}) custom-call(s32[2]{0:T(128)} %clips_h.1, s32[2]{0:T(128)} %owners_h.1, s32[2]{0:T(128)} %slots_h.1, bf16[2,64,256]{2,1,0:T(8,128)(2,1)} %bitcast.5, ...), custom_call_target="tpu_custom_call" | custom-call | tf_op jit(solution)/shard_map/routing/pallas_call | solution.py:275
  26.3 6.2 %finish.1 = (bf16[1024,768]{1,0:T(8,128)(2,1)}, bf16[1024,768]{1,0:T(8,128)(2,1)}) custom-call(bf16[4,4,16,256]{3,2,1,0:T(8,128)(2,1)S(1)} %get-tuple-element.7.xt, f32[6,288,256]{2,1,0:T(8,128)S(1)} %get-tuple-element.8.m_in, f32[2,4,256,256]{3,2,1,0:T(8,128)S(1)} %get-tuple-element.9.cs, bf16[3,80,80]{2,1,0:T(8,128)(2,1)S(1)} %get-tuple-element.10.gram, ...), custom_call_target="tpu_custom_call" | custom-call | tf_op jit(solution)/shard_map/finish/pallas_call | solution.py:387

commit v4 on v3

--- a/solution.py
+++ b/solution.py
@@ -45,42 +45,47 @@
     clips_h, owners_h, slots_h, latents, extents_h, we_h, be_h, shift_h, scale_h, gq_h, gk_h, table_h, wq, wk,
     xt, m_out, cs, gram_out, use,
     clips, owners, slot_ids, extents, we, be, shift, scale, gq, gk, table, w, left, base, halved,
-    near, tags, frame, wanted, side, side_tags,
-    in_sem, w_sem, s1, r1, t1, u1, s2, r2, t2, u2, s3, r3,
+    mine, near, frame, wanted, side, ready,
+    in_sem, w_sem, s1, r1, s2, r2, s3, r3,
     *, deep, across,
 ):
     me = lax.axis_index("seq")
     x = lax.axis_index("head")
-    heads = xt.shape[0]
-    blocks, share, tokens = near.shape[1:]
+    heads = xt.shape[0] // 2
+    blocks, channels, tokens = latents.shape
+    share = channels // (2 * heads)
+    pair = tokens // 128
     group = 2 * across
-    plane, within = me // group, me % group
-    y, core = within // 2, within % 2
-    own = xt.shape[1]
-    channels, depth = we_h.shape
+    plane, y, core = me // group, me % group // 2, me % 2
+    own = 2 * blocks
+    both = 2 * own
+    depth = we_h.shape[1]
     per = w.shape[0] // 2
 
-    def z_peer(r):
-        return {"seq": (plane + r) % deep * group + within}
+    def z_peer(q):
+        return {"seq": ((plane + q // 2) % deep * across + y) * 2 + (core + q) % 2}
 
     def y_peer(r):
-        return {"seq": plane * group + (y + r // 2) % across * 2 + (core + r) % 2}
-
-    def x_peer(r):
-        return {"head": (x + r) % heads}
-
-    z_steps = sorted(range(1, deep), key=lambda r: -min(r, deep - r))
-    y_steps = sorted(range(1, group), key=lambda r: -min(r // 2, across - r // 2))
-    x_steps = sorted(range(1, heads), key=lambda r: -min(r, heads - r))
+        return {"seq": (plane * across + (y + r) % across) * 2 + core}
+
+    def x_peer(q):
+        return {"seq": me - core + (core + q) % 2, "head": (x + q // 2) % heads}
+
+    z_steps = sorted(range(1, 2 * deep), key=lambda q: -min(q // 2, deep - q // 2))
+    y_steps = sorted(range(1, across), key=lambda r: -min(r, across - r))
+    x_steps = sorted(range(1, 2 * heads), key=lambda q: -min(q // 2, heads - q // 2))
+    peers = [z_peer(q) for q in z_steps] + [y_peer(r) for r in y_steps] + [x_peer(q) for q in x_steps if q != 1]
     barrier = pltpu.get_barrier_semaphore()
-    for peer in [z_peer(r) for r in z_steps] + [y_peer(r) for r in y_steps] + [x_peer(r) for r in x_steps]:
+    for peer in peers:
         pl.semaphore_signal(barrier, inc=1, device_id=peer, device_id_type=MESH)
 
     takes = [
         pltpu.make_async_copy(source, place, in_sem.at[k])
         for k, (source, place) in enumerate((
             (clips_h, clips), (owners_h, owners), (slots_h, slot_ids),
-            (latents.at[:, pl.ds(x * share, share), :], near.at[0]),
+            *((latents.at[:, pl.ds(pl.multiple_of((2 * x + (core + k) % 2) * share, share), share),
+                          h * 128 : (h + 1) * 128],
+               mine.at[k, h * blocks : (h + 1) * blocks]) for k in range(2) for h in range(pair)),
             (we_h, we), (be_h, be), (gq_h, gq), (gk_h, gk), (table_h, table),
             (shift_h, shift), (scale_h, scale), (extents_h, extents),
         ))
@@ -91,13 +96,14 @@
     ]
     for copy in takes + weights:
         copy.start()
+    first = 3 + 2 * pair
 
     sub = lax.broadcasted_iota(I32, (8, 128), 0)
     lane = lax.broadcasted_iota(I32, (8, 128), 1)
-    for r in range(group):
-        for s in range(own):
-            code = y_peer(r)["seq"] * own + s
-            wanted[r * own + s] = jnp.full((share, tokens), code, I32).astype(F32).astype(BF16)
+    for r in range(across):
+        for s in range(both):
+            code = (plane * across + (y + r) % across) * both + s
+            wanted[r, s] = jnp.full((share, 128), code, I32).astype(F32).astype(BF16)
     for copy in takes[:3]:
         copy.wait()
     tag = jnp.zeros((8, 128), I32)
@@ -107,34 +113,39 @@
         tag = tag + jnp.where(here & (sub == 0), clips[j], 0)
         tag = tag + jnp.where(here & (sub == 1), code, 0)
         tag = tag + jnp.where(sub == 2 + j, code, 0)
-    tags[0] = tag
-    takes[3].wait()
-    pl.semaphore_wait(barrier, deep + group + heads - 3)
-
-    def z_copies(r):
-        return (
-            pltpu.make_async_remote_copy(
-                near.at[0], near.at[r], s1.at[r], r1.at[r], device_id=z_peer(r), device_id_type=MESH),
-            pltpu.make_async_remote_copy(
-                tags.at[0], tags.at[r], t1.at[r], u1.at[r], device_id=z_peer(r), device_id_type=MESH),
-        )
+    tag = tag.astype(F32)
+    mine[0, pair * blocks] = tag.astype(BF16)
+    mine[1, pair * blocks] = tag.astype(BF16)
+    for copy in takes[3:first]:
+        copy.wait()
+    pl.semaphore_wait(barrier, len(peers))
+
+    def z_copy(q):
+        return pltpu.make_async_remote_copy(
+            mine.at[q % 2], near.at[q], s1.at[q], r1.at[q], device_id=z_peer(q), device_id_type=MESH)
 
     sent = []
-    for r in z_steps:
-        data, words = z_copies(r)
-        data.start()
-        words.start()
-        sent += [data, words]
-
-    def sort_in(r, first):
-        for j in range(blocks):
-            code = jnp.broadcast_to(tags[r, 2 + j : 3 + j, :], (share, 128)).astype(F32).astype(BF16)
-            code = jnp.concatenate([code] * (tokens // 128), axis=1)
-            hit = wanted[...] == code[None]
-            before = jnp.zeros(frame.shape, BF16) if first and j == 0 else frame[...]
-            frame[...] = jnp.where(hit, near[r, j][None], before)
-
-    for copy in takes[4:]:
+    for q in z_steps:
+        copy = z_copy(q)
+        copy.start()
+        sent.append(copy)
+
+    def sort_in(sources, fresh):
+        tags = [source[pair * blocks].astype(F32) for source in sources]
+        codes = [
+            (source, j, jnp.broadcast_to(words[2 + j : 3 + j, :], (share, 128)).astype(BF16))
+            for source, words in zip(sources, tags) for j in range(blocks)
+        ]
+        for r in range(across):
+            for h in range(pair):
+                at = pl.ds(h * both, both)
+                held = jnp.zeros((both, share, 128), BF16) if fresh else frame[r, at]
+                for source, j, code in codes:
+                    held = jnp.where(wanted[r] == code[None], source[h * blocks + j][None], held)
+                frame[r, at] = held
+        return sum(tags[1:], tags[0])
+
+    for copy in takes[first:]:
         copy.wait()
     a = we[...].astype(F32)
     a = a - jnp.mean(a, axis=1, keepdims=True)
@@ -156,48 +167,44 @@
         halved[k, 0:128, :] = hi
         halved[k, 128:256, :] = lo
 
-    sort_in(0, True)
-    total = tags[0]
-    for r in reversed(z_steps):
-        data, words = z_copies(r)
-        data.wait_recv()
-        words.wait_recv()
-        sort_in(r, False)
-        total = total + tags[r]
-    side_tags[0] = total
-
-    def y_copies(r):
-        return (
-            pltpu.make_async_remote_copy(
-                frame.at[pl.ds(r * own, own)], side.at[r], s2.at[r], r2.at[r],
-                device_id=y_peer(r), device_id_type=MESH),
-            pltpu.make_async_remote_copy(
-                side_tags.at[0], side_tags.at[r], t2.at[r], u2.at[r],
-                device_id=y_peer(r), device_id_type=MESH),
-        )
-
+    z_copy(1).wait_recv()
+    total = sort_in([mine.at[0], near.at[1]], True)
+    for r in range(1, deep // 2 + 1):
+        for q in sorted({2 * r, 2 * r + 1, 2 * (deep - r), 2 * (deep - r) + 1}):
+            z_copy(q).wait_recv()
+        for r_one in sorted({r, deep - r}):
+            total = total + sort_in([near.at[2 * r_one], near.at[2 * r_one + 1]], False)
     for r in y_steps:
-        data, words = y_copies(r)
-        words.start()
-        data.start()
-        sent += [data, words]
-    mine = frame[0:own]
-    for r in reversed(y_steps):
-        data, words = y_copies(r)
-        data.wait_recv()
-        words.wait_recv()
-        mine = mine + side[r]
-        total = total + side_tags[r]
-    xt[x] = mine
-
-    def x_copy(r):
+        frame[r, pair * both] = total.astype(BF16)
+
+    def y_copy(r):
         return pltpu.make_async_remote_copy(
-            xt.at[x], xt.at[x], s3.at[r], r3.at[r], device_id=x_peer(r), device_id_type=MESH)
-
-    for r in x_steps:
-        copy = x_copy(r)
+            frame.at[r], side.at[r], s2.at[r], r2.at[r], device_id=y_peer(r), device_id_type=MESH)
+
+    for r in y_steps:
+        copy = y_copy(r)
         copy.start()
         sent.append(copy)
+    whole = frame[0, 0 : pair * both]
+    for r in reversed(y_steps):
+        y_copy(r).wait_recv()
+        whole = whole + side[r, 0 : pair * both]
+        total = total + side[r, pair * both].astype(F32)
+    for c in range(2):
+        for h in range(pair):
+            ready[c, h * own : (h + 1) * own] = whole[h * both + c * own : h * both + (c + 1) * own]
+    spot = 2 * x + core
+
+    def x_copy(q):
+        return pltpu.make_async_remote_copy(
+            ready.at[(core + q) % 2], xt.at[spot], s3.at[q], r3.at[q], device_id=x_peer(q), device_id_type=MESH)
+
+    for q in x_steps:
+        copy = x_copy(q)
+        copy.start()
+        sent.append(copy)
+    xt[spot] = ready[core]
+    total = total.astype(I32)
 
     clip_row = jnp.broadcast_to(total[0:1, :], (8, 128))
     found = jnp.broadcast_to(total[1:2, :], (8, 128)) == me * own + sub
@@ -249,10 +256,10 @@
         cs[0, s] = jnp.dot(hot, halved[0], preferred_element_type=F32)
         cs[1, s] = jnp.dot(hot, halved[1], preferred_element_type=F32)
 
-    for r in reversed(x_steps):
-        at = xt.at[(x + heads - r) % heads]
+    for q in reversed(x_steps):
+        at = xt.at[(x + heads - q // 2) % heads * 2 + (core + q) % 2]
         pltpu.make_async_remote_copy(
-            at, at, s3.at[r], r3.at[r], device_id=x_peer(r), device_id_type=MESH).wait_recv()
+            at, at, s3.at[q], r3.at[q], device_id=x_peer(q), device_id_type=MESH).wait_recv()
     for copy in sent:
         copy.wait_send()
 
@@ -263,8 +270,8 @@
     blocks, channels, tokens = latents.shape
     own = 2 * blocks
     heads, deep = lax.axis_size("head"), lax.axis_size("seq") // (2 * across)
-    share = channels // heads
-    group = 2 * across
+    share, pair = channels // (2 * heads), tokens // 128
+    both = 2 * own
     depth, columns = wq.shape
     chunks = 2 * columns // WIDE
     dma, room = pltpu.SemaphoreType.DMA, pltpu.VMEM
@@ -275,7 +282,7 @@
     return pl.pallas_call(
         functools.partial(routing_kernel, deep=deep, across=across),
         out_shape=[
-            jax.ShapeDtypeStruct((heads, own, share, tokens), BF16),
+            jax.ShapeDtypeStruct((2 * heads, pair * own, share, 128), BF16),
             jax.ShapeDtypeStruct((chunks, rows, WIDE), F32),
             jax.ShapeDtypeStruct((2, own, tokens, 256), F32),
             jax.ShapeDtypeStruct((3, channels + 16, channels + 16), BF16),
@@ -290,16 +297,14 @@
             room((rows, depth), BF16),
             room((channels + 16, depth), F32),
             room((2, 256, 256), BF16),
-            room((deep, blocks, share, tokens), BF16),
-            room((deep, 8, 128), I32),
-            room((group * own, share, tokens), BF16),
-            room((group * own, share, tokens), BF16),
-            room((group, own, share, tokens), BF16),
-            room((group, 8, 128), I32),
-            dma((12,)), dma((chunks,)),
-            dma((deep,)), dma((deep,)), dma((deep,)), dma((deep,)),
-            dma((group,)), dma((group,)), dma((group,)), dma((group,)),
-            dma((heads,)), dma((heads,)),
+            room((2, pair * blocks + 1, share, 128), BF16),
+            room((2 * deep, pair * blocks + 1, share, 128), BF16),
+            room((across, pair * both + 1, share, 128), BF16),
+            room((across, both, share, 128), BF16),
+            room((across, pair * both + 1, share, 128), BF16),
+            room((2, pair * own, share, 128), BF16),
+            dma((11 + 2 * pair,)), dma((chunks,)),
+            dma((2 * deep,)), dma((2 * deep,)), dma((across,)), dma((across,)), dma((2 * heads,)), dma((2 * heads,)),
         ],
         compiler_params=pltpu.CompilerParams(
             collective_id=0, has_side_effects=True, vmem_limit_bytes=28 << 20),
@@ -308,29 +313,38 @@
 
 
 def finish_kernel(xt, m_in, cs, gram, use, oq, ok, zz, eps, out, o_sem):
-    heads, slots, share, tokens = xt.shape
-    channels = heads * share
+    parts, both, share, _ = xt.shape
+    slots, tokens = zz.shape[:2]
+    pair = both // slots
+    channels = parts * share
     chunks, _, wide = m_in.shape
     per = chunks // 2
     sub = lax.broadcasted_iota(I32, (16, tokens), 0)
+    e_row = lax.broadcasted_iota(I32, (128, 128), 0)
+    spread = jnp.where((e_row == channels + 3) | (e_row == channels + 4), 1.0, 0.0).astype(BF16)
     for s in range(slots):
-        x = jnp.concatenate([xt[h, s] for h in range(heads)], axis=0)
-        x1 = jnp.concatenate([x, jnp.where(sub == 0, 1.0, 0.0).astype(BF16)], axis=0)
+        xf = jnp.concatenate(
+            [jnp.concatenate([xt[p, h * slots + s].astype(F32) for h in range(pair)], axis=1)
+             for p in range(parts)], axis=0)
+        x1f = jnp.concatenate([xf, jnp.where(sub == 0, 1.0, 0.0)], axis=0)
+        x1 = x1f.astype(BF16)
         y = sum(jnp.dot(gram[k], x1, preferred_element_type=F32) for k in range(3))
-        xf = x1.astype(F32)
-        var = jnp.maximum(jnp.sum(y * xf, axis=0, keepdims=True), 0.0) + 1e-06
+        var = jnp.maximum(jnp.sum(y * x1f, axis=0, keepdims=True), 0.0) + 1e-06
         dev = jnp.sqrt(var)
         dev_hi = dev.astype(BF16).astype(F32)
+        small = var * 1e-06
+        small_hi = small.astype(BF16).astype(F32)
+        live = jnp.concatenate([use[s : s + 1, :]] * (tokens // 128), axis=1)
         more = jnp.where(
-            sub == 0, 1.0,
-            jnp.where(sub == 1, dev_hi,
-                      jnp.where(sub == 2, dev - dev_hi, jnp.where(sub == 3, var * 1e-06, 0.0))),
+            sub == 0, live,
+            jnp.where(sub == 1, dev_hi * live,
+                      jnp.where(sub == 2, (dev - dev_hi) * live,
+                                jnp.where(sub == 3, small_hi, jnp.where(sub == 4, small - small_hi, 0.0)))),
         )
-        zt = jnp.concatenate([xf[0:channels], more, jnp.zeros((112 - channels, tokens), F32)], axis=0)
-        z = zt.T
-        eps[s] = jnp.broadcast_to(z[:, channels + 3 : channels + 4], (tokens, 128))
-        zb = (z * use[s : s + 1, :]).astype(BF16)
-        zz[s] = jnp.concatenate([zb, zb], axis=1)
+        zt = jnp.concatenate([xf, more, jnp.zeros((112 - channels, tokens), F32)], axis=0)
+        z = zt.astype(BF16).T
+        eps[s] = jnp.dot(z, spread, preferred_element_type=F32)
+        zz[s] = jnp.concatenate([z, z], axis=1)
 
     r_i = lax.broadcasted_iota(I32, (wide, wide), 0) // 128
     c_i = lax.broadcasted_iota(I32, (wide, wide), 1) // 128
@@ -348,8 +362,7 @@
         return pltpu.make_async_copy(
             out.at[n], place.at[:, pl.ds(n % per * wide, wide)], o_sem.at[n])
 
-    def chunk(n, carry):
-        which = n // per
+    def chunk(n):
         m = m_in[n]
         turned = lane_swapped(m)
         for s in range(slots):
@@ -357,31 +370,23 @@
             v = jnp.dot(z, stack(m, s), preferred_element_type=F32)
             vs = jnp.dot(z, stack(turned, s), preferred_element_type=F32)
             power = jnp.dot((v * v).astype(BF16), ones, preferred_element_type=F32)
-            c = cs[which, s, :, 0:128]
-            sn = cs[which, s, :, 128:256]
+            c = cs[n // per, s, :, 0:128]
+            sn = cs[n // per, s, :, 128:256]
             e = eps[s]
             for h in range(wide // 128):
                 at = slice(h * 128, (h + 1) * 128)
                 o = (v[:, at] * c + vs[:, at] * sn) * lax.rsqrt(power[:, at] + e)
                 out[n, s * tokens : (s + 1) * tokens, at] = o.astype(BF16)
-
-        @pl.when(n < per)
-        def _():
-            out_copy(n, oq).start()
-
-        @pl.when(n >= per)
-        def _():
-            out_copy(n, ok).start()
-
-        return carry
-
-    lax.fori_loop(0, chunks, chunk, 0)
+        out_copy(n, oq if n < per else ok).start()
+
+    for n in range(chunks):
+        chunk(n)
     for n in range(chunks):
         out_copy(n, oq if n < per else ok).wait()
 
 
 def finished(xt, m, cs, gram, use):
-    heads, slots, share, tokens = xt.shape
+    slots, tokens = cs.shape[1:3]
     chunks, _, wide = m.shape
     rows = slots * tokens
     return pl.pallas_call(

time: 32.6 us -> 31.5 us (0.966)
  Pallas kernels: 31.9 us -> 30.8 us
    pallas_call x1, Pallas kernels: 6.22 us -> 5.45 us  [finished(): pl.pallas_call(finish_kernel, out_shape=[jax.ShapeDtypeStruct((rows, chun...]
    pallas_call x1, Pallas kernels: 25.7 us -> 25.4 us  [routed(): pl.pallas_call(functools.partial(routing_kernel, deep=deep, across=across...]
where the time goes in v4:
time: 31.5 us; the launch traced here: 31.4 us
  Pallas kernels  30.8 us (98%)
  between operations  0.64 us (2%)
    pallas_call x1, Pallas kernels, routed(): pl.pallas_call(functools.partial(routing_kernel, deep=deep, across=across...  25.4 us
    pallas_call x1, Pallas kernels, finished(): pl.pallas_call(finish_kernel, out_shape=[jax.ShapeDtypeStruct((rows, chun...  5.45 us

profile of v4, /device:TPU:1, one launch (start us, length us, event | category | flops | bytes accessed | tf_op | source)
XLA Modules:
  0.0 31.4 jit_solution(745326440445980824)
XLA Ops:
  0.6 25.4 %routing.1 = (bf16[8,8,8,128]{3,2,1,0:T(8,128)(2,1)S(1)}, f32[6,288,256]{2,1,0:T(8,128)S(1)}, f32[2,4,256,256]{3,2,1,0:T(8,128)S(1)}, bf16[3,80,80]{2,1,0:T(8,128)(2,1)S(1)}, f32[8,128]{1,0:T(8,128)S(1)}) custom-call(s32[2]{0:T(128)} %clips_h.1, s32[2]{0:T(128)} %owners_h.1, s32[2]{0:T(128)} %slots_h.1, bf16[2,64,256]{2,1,0:T(8,128)(2,1)} %bitcast.5, ...), custom_call_target="tpu_custom_call" | custom-call | tf_op jit(solution)/shard_map/routing/pallas_call | solution.py:282
  26.0 5.4 %finish.1 = (bf16[1024,768]{1,0:T(8,128)(2,1)}, bf16[1024,768]{1,0:T(8,128)(2,1)}) custom-call(bf16[8,8,8,128]{3,2,1,0:T(8,128)(2,1)S(1)} %get-tuple-element.7.xt, f32[6,288,256]{2,1,0:T(8,128)S(1)} %get-tuple-element.8.m_in, f32[2,4,256,256]{3,2,1,0:T(8,128)S(1)} %get-tuple-element.9.cs, bf16[3,80,80]{2,1,0:T(8,128)(2,1)S(1)} %get-tuple-element.10.gram, ...), custom_call_target="tpu_custom_call" | custom-call | tf_op jit(solution)/shard_map/finish/pallas_call | solution.py:392

commit v5 on v4

--- a/solution.py
+++ b/solution.py
@@ -43,8 +43,8 @@
 
 def routing_kernel(
     clips_h, owners_h, slots_h, latents, extents_h, we_h, be_h, shift_h, scale_h, gq_h, gk_h, table_h, wq, wk,
-    xt, m_out, cs, gram_out, use,
-    clips, owners, slot_ids, extents, we, be, shift, scale, gq, gk, table, w, left, base, halved,
+    xt, stacks, cs, gram_out, use,
+    clips, owners, slot_ids, extents, we, be, shift, scale, gq, gk, table, w, left, held, base, halved,
     mine, near, frame, wanted, side, ready,
     in_sem, w_sem, s1, r1, s2, r2, s3, r3,
     *, deep, across,
@@ -74,11 +74,7 @@
     z_steps = sorted(range(1, 2 * deep), key=lambda q: -min(q // 2, deep - q // 2))
     y_steps = sorted(range(1, across), key=lambda r: -min(r, across - r))
     x_steps = sorted(range(1, 2 * heads), key=lambda q: -min(q // 2, heads - q // 2))
-    peers = [z_peer(q) for q in z_steps] + [y_peer(r) for r in y_steps] + [x_peer(q) for q in x_steps if q != 1]
-    barrier = pltpu.get_barrier_semaphore()
-    for peer in peers:
-        pl.semaphore_signal(barrier, inc=1, device_id=peer, device_id_type=MESH)
-
+    first = 3 + 2 * pair
     takes = [
         pltpu.make_async_copy(source, place, in_sem.at[k])
         for k, (source, place) in enumerate((
@@ -94,16 +90,15 @@
         pltpu.make_async_copy(source.at[:, pl.ds(n * WIDE, WIDE)], w.at[k * per + n], w_sem.at[k * per + n])
         for n in range(per) for k, source in enumerate((wq, wk))
     ]
-    for copy in takes + weights:
+    for copy in takes[:first]:
         copy.start()
-    first = 3 + 2 * pair
+    peers = [z_peer(q) for q in z_steps] + [y_peer(r) for r in y_steps] + [x_peer(q) for q in x_steps if q != 1]
+    barrier = pltpu.get_barrier_semaphore()
+    for peer in peers:
+        pl.semaphore_signal(barrier, inc=1, device_id=peer, device_id_type=MESH)
 
     sub = lax.broadcasted_iota(I32, (8, 128), 0)
     lane = lax.broadcasted_iota(I32, (8, 128), 1)
-    for r in range(across):
-        for s in range(both):
-            code = (plane * across + (y + r) % across) * both + s
-            wanted[r, s] = jnp.full((share, 128), code, I32).astype(F32).astype(BF16)
     for copy in takes[:3]:
         copy.wait()
     tag = jnp.zeros((8, 128), I32)
@@ -129,6 +124,13 @@
         copy = z_copy(q)
         copy.start()
         sent.append(copy)
+
+    for copy in takes[first:] + weights:
+        copy.start()
+    for r in range(across):
+        for s in range(both):
+            code = (plane * across + (y + r) % across) * both + s
+            wanted[r, s] = jnp.full((share, 128), code, I32).astype(F32).astype(BF16)
 
     def sort_in(sources, fresh):
         tags = [source[pair * blocks].astype(F32) for source in sources]
@@ -163,7 +165,7 @@
         gram = gram - part.astype(F32)
     for k, g in enumerate((gq, gk)):
         gain = jnp.concatenate([g[...], lane_swapped(g[...])], axis=1)
-        hi, lo = halves(table[...] * gain)
+        hi, lo = halves(table[...] * (gain * 128.0**0.5))
         halved[k, 0:128, :] = hi
         halved[k, 128:256, :] = lo
 
@@ -227,17 +229,42 @@
         gain = gains[s : s + 1, :]
         left[s * channels : (s + 1) * channels, :] = (base[0:channels, :] * gain).astype(BF16)
         middle = base[channels : channels + 1, :] * gain
-        extra.append(jnp.where(sub8 == 0, middle, jnp.where(sub8 <= 2, moves[s : s + 1, :], 0.0)))
+        extra.append(jnp.where((sub8 == 0) | (sub8 == 3), middle, jnp.where(sub8 <= 4, moves[s : s + 1, :], 0.0)))
     left[own * channels :, :] = jnp.concatenate(extra, axis=0).astype(BF16)
     for copy in weights:
         copy.wait()
 
-    def project(n, carry):
-        m_out[n] = jnp.dot(left[...], w[n], preferred_element_type=F32)
-        m_out[n + per] = jnp.dot(left[...], w[n + per], preferred_element_type=F32)
+    late = lax.broadcasted_iota(I32, (16, WIDE), 0) >= 3
+    blank = jnp.zeros((8, WIDE), F32)
+
+    def place(m, n, k):
+        hi, lo = halves(m[0 : own * channels])
+        for s in range(own):
+            rows = slice(s * channels, (s + 1) * channels)
+            stacks[n, s, k, 0:channels, :] = hi[rows]
+            stacks[n, s, k, channels : 2 * channels, :] = lo[rows]
+            tail = jnp.concatenate([m[own * channels + 8 * s : own * channels + 8 * s + 8], blank], axis=0)
+            over = tail - tail.astype(BF16).astype(F32)
+            stacks[n, s, k, 2 * channels :, :] = jnp.where(late, over, tail).astype(BF16)
+
+    def products(n):
+        for k in range(2):
+            held[k] = jnp.dot(left[...], w[n + k * per], preferred_element_type=F32)
+
+    def placed(n):
+        for k in range(2):
+            m = held[k]
+            place(m, n + k * per, 0)
+            place(lane_swapped(m), n + k * per, 1)
+
+    def both_at(n, carry):
+        placed((n + per - 1) % per)
+        products(n)
         return carry
 
-    lax.fori_loop(0, per, project, 0)
+    held[...] = jnp.zeros_like(held)
+    lax.fori_loop(0, per, both_at, 0)
+    placed(per - 1)
 
     lane_f = lax.broadcasted_iota(I32, (1, 128), 1).astype(F32)
     steps = lax.broadcasted_iota(I32, (tokens, 128), 0).astype(F32)
@@ -283,7 +310,7 @@
         functools.partial(routing_kernel, deep=deep, across=across),
         out_shape=[
             jax.ShapeDtypeStruct((2 * heads, pair * own, share, 128), BF16),
-            jax.ShapeDtypeStruct((chunks, rows, WIDE), F32),
+            jax.ShapeDtypeStruct((chunks, own, 2, 2 * channels + 16, WIDE), BF16),
             jax.ShapeDtypeStruct((2, own, tokens, 256), F32),
             jax.ShapeDtypeStruct((3, channels + 16, channels + 16), BF16),
             jax.ShapeDtypeStruct((8, 128), F32),
@@ -295,6 +322,7 @@
             *(room(v.shape, v.dtype) for v in (args[4], we, flat[0], shift, scale, flat[1], flat[2], table)),
             room((chunks, depth, WIDE), BF16),
             room((rows, depth), BF16),
+            room((2, rows, WIDE), F32),
             room((channels + 16, depth), F32),
             room((2, 256, 256), BF16),
             room((2, pair * blocks + 1, share, 128), BF16),
@@ -312,16 +340,16 @@
     )(*(pltpu.with_memory_space_constraint(v, pltpu.HBM) for v in args))
 
 
-def finish_kernel(xt, m_in, cs, gram, use, oq, ok, zz, eps, out, o_sem):
+def finish_kernel(xt, stacks, cs, gram, use, oq, ok, zz, eps, out, o_sem):
     parts, both, share, _ = xt.shape
     slots, tokens = zz.shape[:2]
     pair = both // slots
     channels = parts * share
-    chunks, _, wide = m_in.shape
+    chunks, _, _, deep, wide = stacks.shape
     per = chunks // 2
     sub = lax.broadcasted_iota(I32, (16, tokens), 0)
-    e_row = lax.broadcasted_iota(I32, (128, 128), 0)
-    spread = jnp.where((e_row == channels + 3) | (e_row == channels + 4), 1.0, 0.0).astype(BF16)
+    e_row = lax.broadcasted_iota(I32, (deep, 128), 0)
+    spread = jnp.where(e_row // 2 == channels + 3, 1.0, 0.0).astype(BF16)
     for s in range(slots):
         xf = jnp.concatenate(
             [jnp.concatenate([xt[p, h * slots + s].astype(F32) for h in range(pair)], axis=1)
@@ -332,50 +360,32 @@
         var = jnp.maximum(jnp.sum(y * x1f, axis=0, keepdims=True), 0.0) + 1e-06
         dev = jnp.sqrt(var)
         dev_hi = dev.astype(BF16).astype(F32)
-        small = var * 1e-06
+        small = var * (128.0 * 1e-06)
         small_hi = small.astype(BF16).astype(F32)
         live = jnp.concatenate([use[s : s + 1, :]] * (tokens // 128), axis=1)
-        more = jnp.where(
-            sub == 0, live,
-            jnp.where(sub == 1, dev_hi * live,
-                      jnp.where(sub == 2, (dev - dev_hi) * live,
-                                jnp.where(sub == 3, small_hi, jnp.where(sub == 4, small - small_hi, 0.0)))),
-        )
-        zt = jnp.concatenate([xf, more, jnp.zeros((112 - channels, tokens), F32)], axis=0)
+        more = jnp.where((sub == 1) | (sub == 4), dev_hi, jnp.where(sub == 2, dev - dev_hi, 1.0)) * live
+        more = jnp.where(sub < 5, more, jnp.where(sub == 6, small_hi, jnp.where(sub == 7, small - small_hi, 0.0)))
+        zt = jnp.concatenate([xf, xf, more], axis=0)
         z = zt.astype(BF16).T
         eps[s] = jnp.dot(z, spread, preferred_element_type=F32)
-        zz[s] = jnp.concatenate([z, z], axis=1)
-
-    r_i = lax.broadcasted_iota(I32, (wide, wide), 0) // 128
-    c_i = lax.broadcasted_iota(I32, (wide, wide), 1) // 128
-    ones = jnp.where(r_i == c_i, 1.0 / 128.0, 0.0).astype(BF16)
-    empty = jnp.zeros((128 - channels - 8, wide), F32)
-
-    def stack(m, s):
-        own = jnp.concatenate(
-            [m[s * channels : (s + 1) * channels],
-             m[slots * channels + 8 * s : slots * channels + 8 * s + 8], empty], axis=0)
-        hi, lo = halves(own)
-        return jnp.concatenate([hi, lo], axis=0)
+        zz[s] = z
 
     def out_copy(n, place):
         return pltpu.make_async_copy(
             out.at[n], place.at[:, pl.ds(n % per * wide, wide)], o_sem.at[n])
 
     def chunk(n):
-        m = m_in[n]
-        turned = lane_swapped(m)
         for s in range(slots):
             z = zz[s]
-            v = jnp.dot(z, stack(m, s), preferred_element_type=F32)
-            vs = jnp.dot(z, stack(turned, s), preferred_element_type=F32)
-            power = jnp.dot((v * v).astype(BF16), ones, preferred_element_type=F32)
+            v = jnp.dot(z, stacks[n, s, 0], preferred_element_type=F32)
+            vs = jnp.dot(z, stacks[n, s, 1], preferred_element_type=F32)
             c = cs[n // per, s, :, 0:128]
             sn = cs[n // per, s, :, 128:256]
             e = eps[s]
             for h in range(wide // 128):
                 at = slice(h * 128, (h + 1) * 128)
-                o = (v[:, at] * c + vs[:, at] * sn) * lax.rsqrt(power[:, at] + e)
+                power = jnp.sum(v[:, at] * v[:, at], axis=1, keepdims=True)
+                o = (v[:, at] * c + vs[:, at] * sn) * lax.rsqrt(power + e)
                 out[n, s * tokens : (s + 1) * tokens, at] = o.astype(BF16)
         out_copy(n, oq if n < per else ok).start()
 
@@ -385,9 +395,9 @@
         out_copy(n, oq if n < per else ok).wait()
 
 
-def finished(xt, m, cs, gram, use):
+def finished(xt, stacks, cs, gram, use):
     slots, tokens = cs.shape[1:3]
-    chunks, _, wide = m.shape
+    chunks, _, _, deep, wide = stacks.shape
     rows = slots * tokens
     return pl.pallas_call(
         finish_kernel,
@@ -395,14 +405,14 @@
         in_specs=[VMEM] * 5,
         out_specs=[pl.BlockSpec(memory_space=pl.ANY)] * 2,
         scratch_shapes=[
-            pltpu.VMEM((slots, tokens, 256), BF16),
+            pltpu.VMEM((slots, tokens, deep), BF16),
             pltpu.VMEM((slots, tokens, 128), F32),
             pltpu.VMEM((chunks, rows, wide), BF16),
             pltpu.SemaphoreType.DMA((chunks,)),
         ],
         compiler_params=pltpu.CompilerParams(vmem_limit_bytes=28 << 20),
         name="finish",
-    )(xt, m, cs, gram, use)
+    )(xt, stacks, cs, gram, use)
 
 
 def per_device(

time: 31.5 us -> 30.1 us (0.956)
  Pallas kernels: 30.8 us -> 29.4 us
    pallas_call x1, Pallas kernels: 5.45 us -> 3.7 us  [finished(): pl.pallas_call(finish_kernel, out_shape=[jax.ShapeDtypeStruct((rows, chun...]
    pallas_call x1, Pallas kernels: 25.4 us -> 25.7 us  [routed(): pl.pallas_call(functools.partial(routing_kernel, deep=deep, across=across...]
where the time goes in v5:
time: 30.1 us; the launch traced here: 30 us
  Pallas kernels  29.4 us (98%)
  between operations  0.64 us (2%)
    pallas_call x1, Pallas kernels, routed(): pl.pallas_call(functools.partial(routing_kernel, deep=deep, across=across...  25.7 us
    pallas_call x1, Pallas kernels, finished(): pl.pallas_call(finish_kernel, out_shape=[jax.ShapeDtypeStruct((rows, chun...  3.7 us

profile of v5, /device:TPU:1, one launch (start us, length us, event | category | flops | bytes accessed | tf_op | source)
XLA Modules:
  0.0 30.0 jit_solution(5838807259019468529)
XLA Ops:
  0.6 25.7 %routing.1 = (bf16[8,8,8,128]{3,2,1,0:T(8,128)(2,1)S(1)}, bf16[6,4,2,144,256]{4,3,2,1,0:T(8,128)(2,1)S(1)}, f32[2,4,256,256]{3,2,1,0:T(8,128)S(1)}, bf16[3,80,80]{2,1,0:T(8,128)(2,1)S(1)}, f32[8,128]{1,0:T(8,128)S(1)}) custom-call(s32[2]{0:T(128)} %clips_h.1, s32[2]{0:T(128)} %owners_h.1, s32[2]{0:T(128)} %slots_h.1, bf16[2,64,256]{2,1,0:T(8,128)(2,1)} %bitcast.5, ...), custom_call_target="tpu_custom_call" | custom-call | tf_op jit(solution)/shard_map/routing/pallas_call | solution.py:309
  26.3 3.7 %finish.1 = (bf16[1024,768]{1,0:T(8,128)(2,1)}, bf16[1024,768]{1,0:T(8,128)(2,1)}) custom-call(bf16[8,8,8,128]{3,2,1,0:T(8,128)(2,1)S(1)} %get-tuple-element.7.xt, bf16[6,4,2,144,256]{4,3,2,1,0:T(8,128)(2,1)S(1)} %get-tuple-element.8.stacks, f32[2,4,256,256]{3,2,1,0:T(8,128)S(1)} %get-tuple-element.9.cs, bf16[3,80,80]{2,1,0:T(8,128)(2,1)S(1)} %get-tuple-element.10.gram, ...), custom_call_target="tpu_custom_call" | custom-call | tf_op jit(solution)/shard_map/finish/pallas_call | solution.py:402
